TPU v7x, 256 devices: a whole 4x4x8 slice. The times are simulated.
256 devices in a mesh: sec: 8 (over y, core), op: 32 (over z, x).
Axes of the slice: x: 4, y: 4, z: 8, core: 2. Of those that a mesh axis runs over, the one named last changes fastest.
Arguments:
- wavefunction: bfloat16 [8, 512, 1024], P('sec', 'op'), may hold values from -4.5 to 4.5
- op_blocks: bfloat16 [32, 8, 1024, 1024], P('op', 'sec'), may hold values from -6 to 6
- basis_guess: bfloat16 [8, 1024, 512], P('sec'), may hold values from -4.5 to 4.5
- sector_sizes: int32 [8], replicated, may hold values from 768 to 1024
- kept_counts: int32 [8], replicated, may hold values from 256 to 512
- target_map: int32 [32, 8], replicated, may hold values from 0 to 7, as said below
- noise_numerator: int32 [1], replicated, may hold values from 256 to 1024
- noise_denominator: int32 [1], replicated, may hold values from 4194304 to 8388608
Outputs:
- kept_basis: float32 [8, 1024, 512], P('sec', 'op')
- rotated: float32 [32, 8, 512, 512], P('op', 'sec')
Inputs may be any that keep to these rules, and one draw needn't show every extreme that they name: For every operator k, target_map[k] is a permutation of the 8 sectors.
All inputs are finite; a program needn't handle non-finite values.
Results may differ from a plain program's by a relative error of at most 0.005.
Values may be sent and summed in bfloat16 or wider, within the bound.
No kernel may reach another device: no remote copies, remote signals or barrier semaphores. Data moves between devices by JAX's collectives and lax.ppermute only.
A program may use at most 64 MiB of HBM per device.

v0:
```python
import jax
import jax.numpy as jnp
from jax import lax
from jax.sharding import PartitionSpec as P


def from_everyone(value, axis):
    size = lax.axis_size(axis)
    return lax.all_to_all(
        jnp.broadcast_to(value[None], (size, *value.shape)), axis, 0, 0, tiled=True
    )


def laid_out(tiles, dim):
    dims = list(tiles.shape[1:])
    dims[dim] *= tiles.shape[0]
    return jnp.moveaxis(tiles, 0, dim).reshape(dims)


def collect(value, axis, dim):
    tiles = from_everyone(value, axis)
    return laid_out(tiles, dim)


def in_blocks(value, dim, size):
    before, after = (value.shape[:dim], value.shape[dim + 1 :])
    return jnp.moveaxis(value.reshape(*before, size, -1, *after), dim, 0)


def summed_on_arrival(value, axis, dim):
    size = lax.axis_size(axis)
    tiles = lax.all_to_all(in_blocks(value, dim, size), axis, 0, 0, tiled=True)
    return jnp.sum(tiles, axis=0)


def source_sectors(target_map):
    sectors = jnp.arange(target_map.shape[1], dtype=jnp.int32)
    matches = target_map[:, :, None] == sectors[None, None, :]
    return jnp.sum(jnp.where(matches, sectors[None, :, None], 0), axis=1)


def fetch_pieces(own_slice, wanted_all):
    everyone = collect(own_slice, "sec", 0)
    outgoing = jnp.take(everyone, wanted_all, axis=0)
    incoming = lax.all_to_all(outgoing, "op", split_axis=1, concat_axis=1, tiled=True)
    return incoming.reshape(
        incoming.shape[0], incoming.shape[1] * incoming.shape[2], incoming.shape[3]
    )


def body(
    wavefunction,
    op_blocks,
    basis_guess,
    sector_sizes,
    kept_counts,
    target_map,
    noise_numerator,
    noise_denominator,
):
    highest = lax.Precision.HIGHEST
    local_count = wavefunction.shape[0]
    state_count = wavefunction.shape[2]
    kept_width = basis_guess.shape[2]
    tile_rows = state_count // lax.axis_size("op")
    sec_index = lax.axis_index("sec")
    op_index = lax.axis_index("op")
    noise_weight = noise_numerator[0].astype(jnp.float32) / noise_denominator[0].astype(jnp.float32)
    sources = source_sectors(target_map)
    own_sectors = sec_index * local_count + jnp.arange(local_count, dtype=jnp.int32)
    wanted_all = jnp.take(sources, own_sectors, axis=1).T
    wanted = lax.dynamic_index_in_dim(wanted_all, op_index, 1, keepdims=False)
    states = jnp.arange(state_count, dtype=jnp.int32)
    own_sizes = jnp.take(sector_sizes, own_sectors)
    own_mask = states[None, :] < own_sizes[:, None]
    source_mask = states[None, :] < jnp.take(sector_sizes, wanted)[:, None]
    own_kept = (
        jnp.arange(kept_width, dtype=jnp.int32)[None, :]
        < jnp.take(kept_counts, own_sectors)[:, None]
    )
    zero_half = jnp.zeros((), jnp.bfloat16)
    own_rows = jnp.where(own_mask[:, None, :], wavefunction, zero_half)
    moved = fetch_pieces(wavefunction, wanted_all)
    moved = jnp.where(source_mask[:, None, :], moved, zero_half)
    blocks = op_blocks[0]
    perturbed = jnp.einsum(
        "lcx,lxy->lcy", moved, blocks, preferred_element_type=jnp.float32
    ).astype(jnp.bfloat16)
    guess_rows = jnp.where(own_mask[:, :, None], basis_guess, zero_half)
    own_proj = jnp.einsum("lcx,lxk->lck", own_rows, guess_rows, preferred_element_type=jnp.float32)
    perturbed_proj = jnp.einsum(
        "lcx,lxk->lck", perturbed, guess_rows, preferred_element_type=jnp.float32
    )
    own_part = own_rows.astype(jnp.float32)
    perturbed_part = perturbed.astype(jnp.float32)
    contribution = jnp.einsum("lcr,lck->rlk", own_part, own_proj, precision=highest)
    image_rows = summed_on_arrival(
        contribution
        + noise_weight
        * jnp.einsum("lcr,lck->rlk", perturbed_part, perturbed_proj, precision=highest),
        "op",
        0,
    )
    image = jnp.transpose(image_rows, (1, 0, 2))
    row_ids = op_index * tile_rows + jnp.arange(tile_rows, dtype=jnp.int32)
    row_mask = row_ids[None, :] < own_sizes[:, None]
    image = jnp.where(row_mask[:, :, None] & own_kept[:, None, :], image, jnp.float32(0.0))
    full_image = collect(image, "op", 1)
    padding = jnp.where(own_kept, jnp.float32(0.0), jnp.float32(1.0))
    correlation = (
        jnp.einsum("ldk,ldm->lkm", full_image, full_image, precision=highest)
        + padding[:, :, None] * jnp.eye(kept_width, dtype=jnp.float32)[None]
    )
    factor = jnp.linalg.cholesky(correlation)
    new_basis = lax.linalg.triangular_solve(
        factor, full_image, left_side=False, lower=True, transpose_a=True
    )
    kept_tile = (
        lax.dynamic_slice_in_dim(new_basis, op_index * tile_rows, tile_rows, 1)
        * float(state_count) ** 0.5
    )
    basis_half = new_basis.astype(jnp.bfloat16)
    mapped = jnp.einsum(
        "lxy,lyk->lxk", blocks, basis_half, preferred_element_type=jnp.float32
    ).astype(jnp.bfloat16)
    own_tile = lax.dynamic_slice_in_dim(basis_half, op_index * tile_rows, tile_rows, 1)
    source_basis = fetch_pieces(own_tile, wanted_all)
    rotated = jnp.einsum("lxk,lxm->lkm", source_basis, mapped, preferred_element_type=jnp.float32)
    return (kept_tile, rotated[None])


def solution(mesh):
    placed = (
        P("sec", "op", None),
        P("op", "sec", None, None),
        P("sec", None, None),
        P(),
        P(),
        P(),
        P(),
        P(),
    )
    return jax.shard_map(
        body,
        mesh=mesh,
        in_specs=placed,
        out_specs=(P("sec", "op", None), P("op", "sec", None, None)),
        check_vma=False,
    )
```

profile of v0, /device:TPU:2, one launch (start us, length us, event | category | flops | bytes accessed | tf_op | source)
XLA Modules:
  0.0 395.6 jit_solution(13385908602583971793)
XLA Ops:
  2.3 4.5 %all-to-all-start = ((bf16[8,1,16,1024]{3,2,1,0:T(8,128)(2,1)}), bf16[8,1,16,1024]{3,2,1,0:T(8,128)(2,1)S(1)}, u32[]{:S(2)}, u32[]{:S(2)}) async-start(bf16[8,1,16,1024]{3,2,1,0:T(8,128)(2,1)} %broadcast_in_dim.158), calls=%async_computation | async-start | bytes 524288 | tf_op jit(solution)/shard_map/all_to_all | solution.py:9
  7.5 6.8 %all-to-all-done = bf16[8,1,16,1024]{3,2,1,0:T(8,128)(2,1)S(1)} async-done(((bf16[8,1,16,1024]{3,2,1,0:T(8,128)(2,1)}), bf16[8,1,16,1024]{3,2,1,0:T(8,128)(2,1)S(1)}, u32[]{:S(2)}, u32[]{:S(2)}) %all-to-all-start) | async-done | bytes 262176 | tf_op jit(solution)/shard_map/all_to_all | solution.py:9
  16.1 11.6 %all-to-all-start.1 = ((bf16[1,32,16,1024]{3,2,0,1:T(8,128)(2,1)}), bf16[1,32,16,1024]{3,2,0,1:T(8,128)(2,1)S(1)}, u32[]{:S(2)}, u32[]{:S(2)}) async-start(bf16[1,32,16,1024]{3,2,0,1:T(8,128)(2,1)} %bitcast_select_fusion.1), calls=%async_computation.1 | async-start | bytes 2097152 | tf_op jit(solution)/shard_map/all_to_all | solution.py:45
  37.4 17.9 %all-to-all-done.1 = bf16[1,32,16,1024]{3,2,0,1:T(8,128)(2,1)S(1)} async-done(((bf16[1,32,16,1024]{3,2,0,1:T(8,128)(2,1)}), bf16[1,32,16,1024]{3,2,0,1:T(8,128)(2,1)S(1)}, u32[]{:S(2)}, u32[]{:S(2)}) %all-to-all-start.1) | async-done | bytes 1048608 | tf_op jit(solution)/shard_map/all_to_all | solution.py:45
  58.4 3.3 add_bitcast_fusion
  64.6 5.8 %all-to-all-start.2 = ((f32[32,32,1,512]{3,1,2,0:T(8,128)}), f32[32,32,1,512]{3,1,2,0:T(8,128)}, u32[]{:S(2)}, u32[]{:S(2)}) async-start(f32[32,32,1,512]{3,1,2,0:T(8,128)} %bitcast.234), calls=%async_computation.2 | async-start | bytes 4194304 | tf_op jit(solution)/shard_map/all_to_all | solution.py:32
  71.6 48.0 %all-to-all-done.2 = f32[32,32,1,512]{3,1,2,0:T(8,128)} async-done(((f32[32,32,1,512]{3,1,2,0:T(8,128)}), f32[32,32,1,512]{3,1,2,0:T(8,128)}, u32[]{:S(2)}, u32[]{:S(2)}) %all-to-all-start.2) | async-done | bytes 2097184 | tf_op jit(solution)/shard_map/all_to_all | solution.py:32
  123.0 5.8 %all-to-all-start.3 = ((f32[32,1,32,512]{3,2,1,0:T(8,128)}), f32[32,1,32,512]{3,2,1,0:T(8,128)}, u32[]{:S(2)}, u32[]{:S(2)}) async-start(f32[32,1,32,512]{3,2,1,0:T(8,128)} %broadcast_in_dim.162), calls=%async_computation.3 | async-start | bytes 4194304 | tf_op jit(solution)/shard_map/all_to_all | solution.py:9
  128.8 47.3 %all-to-all-done.3 = f32[32,1,32,512]{3,2,1,0:T(8,128)} async-done(((f32[32,1,32,512]{3,2,1,0:T(8,128)}), f32[32,1,32,512]{3,2,1,0:T(8,128)}, u32[]{:S(2)}, u32[]{:S(2)}) %all-to-all-start.3) | async-done | bytes 2097184 | tf_op jit(solution)/shard_map/all_to_all | solution.py:9
  176.1 5.7 %fusion.20 = f32[512,512]{0,1:T(8,128)S(1)} fusion(f32[32,1,32,512]{3,2,1,0:T(8,128)} %all-to-all-done.3, f32[512]{0:T(512)S(1)} %broadcast_select_fusion.7), kind=kOutput, calls=%fused_computation.22 | convolution fusion | flops 3222011904 | bytes 3147776 | tf_op jit(solution)/shard_map/ldk,ldm->lkm/dot_general | solution.py:111
  185.6 11.7 %custom-call.34 = f32[1,128,128]{2,1,0:T(8,128)S(1)} custom-call(f32[1,128,128]{2,1,0:T(8,128)S(1)} %cholesky.267), custom_call_target="Cholesky" | custom-call | tf_op jit(solution)/shard_map/jit(cholesky)/cholesky | solution.py:114
  197.5 9.8 %custom-call.35 = f32[1,1,128,128]{2,3,1,0:T(8,128)S(1)} custom-call(f32[1,1,128,128]{3,2,1,0:T(8,128)S(1)} %get-tuple-element.83), custom_call_target="InvertDiagBlocksLowerTriangular" | custom-call | tf_op jit(solution)/shard_map/jit(cholesky)/cholesky | solution.py:114
  209.8 12.1 %custom-call.36 = f32[1,128,128]{2,1,0:T(8,128)S(1)} custom-call(f32[1,128,128]{2,1,0:T(8,128)S(1)} %cholesky.271), custom_call_target="Cholesky" | custom-call | tf_op jit(solution)/shard_map/jit(cholesky)/cholesky | solution.py:114
  222.0 9.8 %custom-call.37 = f32[1,1,128,128]{2,3,1,0:T(8,128)S(1)} custom-call(f32[1,1,128,128]{3,2,1,0:T(8,128)S(1)} %get-tuple-element.80), custom_call_target="InvertDiagBlocksLowerTriangular" | custom-call | tf_op jit(solution)/shard_map/jit(cholesky)/cholesky | solution.py:114
  233.4 11.7 %custom-call.38 = f32[1,128,128]{2,1,0:T(8,128)S(1)} custom-call(f32[1,128,128]{2,1,0:T(8,128)S(1)} %cholesky.276), custom_call_target="Cholesky" | custom-call | tf_op jit(solution)/shard_map/jit(cholesky)/cholesky | solution.py:114
  245.7 9.8 %custom-call.39 = f32[1,1,128,128]{2,3,1,0:T(8,128)S(1)} custom-call(f32[1,1,128,128]{3,2,1,0:T(8,128)S(1)} %get-tuple-element.77), custom_call_target="InvertDiagBlocksLowerTriangular" | custom-call | tf_op jit(solution)/shard_map/jit(cholesky)/cholesky | solution.py:114
  257.0 11.9 %custom-call.40 = f32[1,128,128]{2,1,0:T(8,128)S(1)} custom-call(f32[1,128,128]{2,1,0:T(8,128)S(1)} %fusion.34), custom_call_target="Cholesky" | custom-call | tf_op jit(solution)/shard_map/jit(cholesky)/cholesky | solution.py:114
  273.8 13.7 %while.5 = (s32[]{:T(128)}, f32[1,512,512]{2,1,0:T(8,128)}, s32[4,2]{0,1:T(2,128)S(1)}, f32[4,1,128,128]{3,2,1,0:T(8,128)}, s32[]{:T(128)}) while((s32[]{:T(128)}, f32[1,512,512]{2,1,0:T(8,128)}, s32[4,2]{0,1:T(2,128)S(1)}, f32[4,1,128,128]{3,2,1,0:T(8,128)}, s32[]{:T(128)}) %tuple.61), condition=%wide.while_cond.4, body=%wide.while_body.4.sunk | while | flops 2 | bytes 132205 | solution.py:115
  287.4 40.1 %custom-call.41 = f32[1,4,128,128]{2,3,1,0:T(8,128)S(1)} custom-call(f32[1,4,128,128]{3,2,1,0:T(8,128)} %bitcast.249), custom_call_target="InvertDiagBlocksLowerTriangular" | custom-call | tf_op jit(solution)/shard_map/triangular_solve | solution.py:115
  337.6 3.9 fusion.27
  344.7 11.6 %all_to_all.30 = bf16[8,1,32,512]{3,2,1,0:T(8,128)(2,1)S(1)} all-to-all(bf16[8,1,32,512]{3,2,1,0:T(8,128)(2,1)S(1)} %broadcast_in_dim.167), channel_id=1, replica_groups=mesh['sec'=8,'op'=32] {'sec'}, dimensions={0} | all-to-all | bytes 524288 | tf_op jit(solution)/shard_map/all_to_all | solution.py:9
  358.1 5.6 %all-to-all-start.5 = ((bf16[1,32,32,512]{3,2,0,1:T(8,128)(2,1)}), bf16[1,32,32,512]{3,2,0,1:T(8,128)(2,1)S(1)}, u32[]{:S(2)}, u32[]{:S(2)}) async-start(bf16[1,32,32,512]{3,2,0,1:T(8,128)(2,1)} %bitcast_select_fusion), calls=%async_computation.5 | async-start | bytes 2097152 | tf_op jit(solution)/shard_map/all_to_all | solution.py:45
  365.5 25.9 %all-to-all-done.5 = bf16[1,32,32,512]{3,2,0,1:T(8,128)(2,1)S(1)} async-done(((bf16[1,32,32,512]{3,2,0,1:T(8,128)(2,1)}), bf16[1,32,32,512]{3,2,0,1:T(8,128)(2,1)S(1)}, u32[]{:S(2)}, u32[]{:S(2)}) %all-to-all-start.5) | async-done | bytes 1048608 | tf_op jit(solution)/shard_map/all_to_all | solution.py:45
  391.4 4.0 %convolution_bitcast_fusion = f32[1,1,512,512]{3,2,1,0:T(8,128)} fusion(bf16[1024,512]{1,0:T(8,128)(2,1)S(1)} %bitcast.245, bf16[1,1,1024,1024]{3,2,1,0:T(8,128)(2,1)S(1)} %copy-done, bf16[1024,128]{0,1:T(8,128)(2,1)} %get-tuple-element.88, bf16[1024,128]{0,1:T(8,128)(2,1)} %get-tuple-element.90, bf16[1024,128]{0,1:T(8,128)(2,1)} %get-tuple-element.92, ...), kind=kOutput, calls=%fused_computation.21 | convolution fusion | flops 1615331328 | bytes 5242880 | tf_op jit(solution)/shard_map/lxk,lxm->lkm/dot_general | solution.py:128
  (89 shorter events, 62.2 us)
Async XLA Ops:
  0.6 54.8 %copy-start = (bf16[1,1,1024,1024]{3,2,1,0:T(8,128)(2,1)S(1)}, bf16[1,1,1024,1024]{3,2,1,0:T(8,128)(2,1)}, u32[]{:S(2)}) copy-start(bf16[1,1,1024,1024]{3,2,1,0:T(8,128)(2,1)} %param.9) | copy-start | bytes 6291460
  2.3 12.0 %all-to-all-start = ((bf16[8,1,16,1024]{3,2,1,0:T(8,128)(2,1)}), bf16[8,1,16,1024]{3,2,1,0:T(8,128)(2,1)S(1)}, u32[]{:S(2)}, u32[]{:S(2)}) async-start(bf16[8,1,16,1024]{3,2,1,0:T(8,128)(2,1)} %broadcast_in_dim.158), calls=%async_computation | async-start | bytes 524288 | tf_op jit(solution)/shard_map/all_to_all | solution.py:9
  14.9 16.7 %copy-start.5 = (s32[8]{0:T(128)S(1)}, s32[8]{0:T(128)}, u32[]{:S(2)}) copy-start(s32[8]{0:T(128)} %param.11) | copy-start | bytes 100
  14.9 18.6 %copy-start.4 = (bf16[1,16,1024]{2,1,0:T(8,128)(2,1)S(1)}, bf16[1,16,1024]{2,1,0:T(8,128)(2,1)}, u32[]{:S(2)}) copy-start(bf16[1,16,1024]{2,1,0:T(8,128)(2,1)} %param.8) | copy-start | bytes 98308
  16.1 39.3 %all-to-all-start.1 = ((bf16[1,32,16,1024]{3,2,0,1:T(8,128)(2,1)}), bf16[1,32,16,1024]{3,2,0,1:T(8,128)(2,1)S(1)}, u32[]{:S(2)}, u32[]{:S(2)}) async-start(bf16[1,32,16,1024]{3,2,0,1:T(8,128)(2,1)} %bitcast_select_fusion.1), calls=%async_computation.1 | async-start | bytes 2097152 | tf_op jit(solution)/shard_map/all_to_all | solution.py:45
  55.5 1.3 copy-start.6
  56.8 1.6 copy-start.1
  64.6 5.8 %copy-start.7 = (s32[8]{0:T(128)S(1)}, s32[8]{0:T(128)}, u32[]{:S(2)}) copy-start(s32[8]{0:T(128)} %param.12) | copy-start | bytes 100
  64.6 55.0 %all-to-all-start.2 = ((f32[32,32,1,512]{3,1,2,0:T(8,128)}), f32[32,32,1,512]{3,1,2,0:T(8,128)}, u32[]{:S(2)}, u32[]{:S(2)}) async-start(f32[32,32,1,512]{3,1,2,0:T(8,128)} %bitcast.234), calls=%async_computation.2 | async-start | bytes 4194304 | tf_op jit(solution)/shard_map/all_to_all | solution.py:32
  123.0 53.2 %all-to-all-start.3 = ((f32[32,1,32,512]{3,2,1,0:T(8,128)}), f32[32,1,32,512]{3,2,1,0:T(8,128)}, u32[]{:S(2)}, u32[]{:S(2)}) async-start(f32[32,1,32,512]{3,2,1,0:T(8,128)} %broadcast_in_dim.162), calls=%async_computation.3 | async-start | bytes 4194304 | tf_op jit(solution)/shard_map/all_to_all | solution.py:9
  184.6 1.0 copy-start.3
  343.2 1.3 copy-start.2
  358.1 33.3 %all-to-all-start.5 = ((bf16[1,32,32,512]{3,2,0,1:T(8,128)(2,1)}), bf16[1,32,32,512]{3,2,0,1:T(8,128)(2,1)S(1)}, u32[]{:S(2)}, u32[]{:S(2)}) async-start(bf16[1,32,32,512]{3,2,0,1:T(8,128)(2,1)} %bitcast_select_fusion), calls=%async_computation.5 | async-start | bytes 2097152 | tf_op jit(solution)/shard_map/all_to_all | solution.py:45
where the time goes:
time: 402 us; the launch traced here: 396 us
  waiting for transfers between devices  146 us (36%)
  other arithmetic  128 us (32%)
  matrix products  39.7 us (10%)
  starting transfers between devices  33.2 us (8%)
  local copies, waits for them, and re-layouts  28.5 us (7%)
  blocking collectives  11.6 us (3%)
  between operations  8.82 us (2%)
    another operation x14, other arithmetic, body(): factor = jnp.linalg.cholesky(correlation)  78.9 us
    all_to_all x2, waiting for transfers between devices, from_everyone(): lax.all_to_all(jnp.broadcast_to(value[None], (size, *value.shape)), axis,...  54.1 us
    all_to_all x1, waiting for transfers between devices, summed_on_arrival(): tiles = lax.all_to_all(in_blocks(value, dim, size), axis, 0, 0, tiled=True)  48 us
    all_to_all x2, waiting for transfers between devices, fetch_pieces(): lax.all_to_all(outgoing, 'op', split_axis=1, concat_axis=1, tiled=True)  43.8 us
    another operation x4, other arithmetic, body(): lax.linalg.triangular_solve(factor, full_image, left_side=False, lower=Tr...  41.5 us
    all_to_all x2, starting transfers between devices, fetch_pieces(): lax.all_to_all(outgoing, 'op', split_axis=1, concat_axis=1, tiled=True)  17.2 us
    another operation x7, matrix products, body(): lax.linalg.triangular_solve(factor, full_image, left_side=False, lower=Tr...  15.3 us
    another operation x12, local copies, waits for them, and re-layouts  13.7 us
  transfers between devices with their start and end apart: 5, of which 5 were waited for; matrix products, arithmetic and copies ran while one was open for 2% of the time, Pallas kernels for 0%

commit v1 on v0

--- a/solution.py
+++ b/solution.py
@@ -1,7 +1,134 @@
 import jax
 import jax.numpy as jnp
 from jax import lax
+from jax.experimental import pallas as pl
+from jax.experimental.pallas import tpu as pltpu
 from jax.sharding import PartitionSpec as P
+
+HI = lax.Precision.HIGHEST
+LANE = 128
+
+def dot(a, b, ca, cb):
+    return lax.dot_general(a, b, (((ca,), (cb,)), ((), ())), precision=HI,
+                           preferred_element_type=jnp.float32)
+
+def factor_block(block):
+    n = LANE
+    sub = lax.broadcasted_iota(jnp.int32, (8, LANE), 0)
+    lane = lax.broadcasted_iota(jnp.int32, (8, LANE), 1)
+    groups = n // 8
+    per = 4
+    rows = [block[8 * g:8 * g + 8, :] for g in range(groups)]
+    aug = [jnp.where(lane == sub + 8 * g, 1.0, 0.0).astype(jnp.float32) for g in range(groups)]
+    out = []
+    for s in range(0, groups, per):
+        done_r, done_w = [], []
+        for g in range(s, s + per):
+            v, w = rows[g], aug[g]
+            cols = [jnp.broadcast_to(v[:, 8 * g + j:8 * g + j + 1], (8, LANE)) for j in range(8)]
+            e = {(i, j): jnp.broadcast_to(cols[j][i:i + 1, :], (8, LANE)) for j in range(8) for i in range(j, 8)}
+            inv, low = [], {}
+            for j in range(8):
+                d = e[j, j]
+                r = lax.rsqrt(d)
+                r = r * (1.5 - 0.5 * d * r * r)
+                inv.append(r)
+                for i in range(j + 1, 8):
+                    low[i, j] = e[i, j] * r
+                for k in range(j + 1, 8):
+                    for i in range(k, 8):
+                        e[i, k] = e[i, k] - low[i, j] * low[k, j]
+            m = {}
+            for c in range(8):
+                m[c, c] = inv[c]
+                for i in range(c + 1, 8):
+                    t = low[i, c] * m[c, c]
+                    for k in range(c + 1, i):
+                        t = t + low[i, k] * m[k, c]
+                    m[i, c] = -t * inv[i]
+            rv = rw = None
+            mcols = []
+            for j in range(8):
+                mc = jnp.zeros((8, LANE), jnp.float32)
+                for i in range(j, 8):
+                    mc = jnp.where(sub == i, m[i, j], mc)
+                tv = mc * jnp.broadcast_to(v[j:j + 1, :], (8, LANE))
+                tw = mc * jnp.broadcast_to(w[j:j + 1, :], (8, LANE))
+                rv = tv if rv is None else rv + tv
+                rw = tw if rw is None else rw + tw
+            out.append(rw)
+            done_r.append(rv)
+            done_w.append(rw)
+            if g + 1 < s + per:
+                rvb = [jnp.broadcast_to(rv[j:j + 1, :], (8, LANE)) for j in range(8)]
+                rwb = [jnp.broadcast_to(rw[j:j + 1, :], (8, LANE)) for j in range(8)]
+                for h in range(g + 1, s + per):
+                    raw = [jnp.broadcast_to(rows[h][:, 8 * g + j:8 * g + j + 1], (8, LANE)) for j in range(8)]
+                    nv, nw = rows[h], aug[h]
+                    for i in range(8):
+                        f = raw[0] * m[i, 0]
+                        for k in range(1, i + 1):
+                            f = f + raw[k] * m[i, k]
+                        nv = nv - f * rvb[i]
+                        nw = nw - f * rwb[i]
+                    rows[h], aug[h] = nv, nw
+        if s + per < groups:
+            left = jnp.concatenate(done_r, axis=0)
+            both = jnp.concatenate([left, jnp.concatenate(done_w, axis=0)], axis=1)
+            rest = 8 * (s + per)
+            delta = dot(left, both, 0, 0)
+            for h in range(s + per, groups):
+                rows[h] = rows[h] - delta[8 * h:8 * h + 8, :LANE]
+                aug[h] = aug[h] - delta[8 * h:8 * h + 8, LANE:]
+    return jnp.concatenate(out, axis=0)
+
+
+def orthogonalize_kernel(kept_ref, corr_ref, image_ref, tile_ref, half_ref, kept_tile_ref, a_ref, q_ref, t_ref):
+    n = corr_ref.shape[0]
+    blocks = n // LANE
+    kept = kept_ref[0]
+    r_i = lax.broadcasted_iota(jnp.int32, (n, n), 0)
+    c_i = lax.broadcasted_iota(jnp.int32, (n, n), 1)
+    a_ref[...] = corr_ref[...] + jnp.where((r_i == c_i) & (c_i >= kept), 1.0, 0.0)
+    scale = float(image_ref.shape[0]) ** 0.5
+    for b in range(blocks):
+        lo, hi = b * LANE, (b + 1) * LANE
+        inv = factor_block(a_ref[lo:hi, lo:hi])
+        for src, dst in ((image_ref, q_ref), (tile_ref, t_ref)):
+            t = src[:, lo:hi]
+            if b:
+                t = t - dot(dst[:, :lo], a_ref[:lo, lo:hi], 1, 0)
+            dst[:, lo:hi] = dot(t, inv, 1, 1)
+        half_ref[:, lo:hi] = q_ref[:, lo:hi].astype(jnp.bfloat16)
+        kept_tile_ref[:, lo:hi] = t_ref[:, lo:hi] * scale
+        if b + 1 < blocks:
+            r = dot(inv, a_ref[lo:hi, hi:], 1, 0)
+            a_ref[lo:hi, hi:] = r
+            for c in range(b + 1, blocks):
+                cl = c * LANE
+                a_ref[cl:cl + LANE, cl:] = a_ref[cl:cl + LANE, cl:] - dot(
+                    r[:, cl - hi:cl - hi + LANE], r[:, cl - hi:], 0, 0)
+
+
+def orthogonalize(corr, image, tile, kept):
+    n = corr.shape[0]
+    vmem = pl.BlockSpec(memory_space=pltpu.VMEM)
+    return pl.pallas_call(
+        orthogonalize_kernel,
+        out_shape=(
+            jax.ShapeDtypeStruct(image.shape, jnp.bfloat16),
+            jax.ShapeDtypeStruct(tile.shape, jnp.float32),
+        ),
+        in_specs=[pl.BlockSpec(memory_space=pltpu.SMEM), vmem, vmem, vmem],
+        out_specs=(vmem, vmem),
+        scratch_shapes=[
+            pltpu.VMEM((n, n), jnp.float32),
+            pltpu.VMEM(image.shape, jnp.float32),
+            pltpu.VMEM(tile.shape, jnp.float32),
+        ],
+        compiler_params=pltpu.CompilerParams(vmem_limit_bytes=40 << 20),
+        name="orthogonalize",
+    )(kept, corr, image, tile)
 
 
 def from_everyone(value, axis):
@@ -106,20 +233,12 @@
     row_mask = row_ids[None, :] < own_sizes[:, None]
     image = jnp.where(row_mask[:, :, None] & own_kept[:, None, :], image, jnp.float32(0.0))
     full_image = collect(image, "op", 1)
-    padding = jnp.where(own_kept, jnp.float32(0.0), jnp.float32(1.0))
-    correlation = (
-        jnp.einsum("ldk,ldm->lkm", full_image, full_image, precision=highest)
-        + padding[:, :, None] * jnp.eye(kept_width, dtype=jnp.float32)[None]
-    )
-    factor = jnp.linalg.cholesky(correlation)
-    new_basis = lax.linalg.triangular_solve(
-        factor, full_image, left_side=False, lower=True, transpose_a=True
-    )
-    kept_tile = (
-        lax.dynamic_slice_in_dim(new_basis, op_index * tile_rows, tile_rows, 1)
-        * float(state_count) ** 0.5
-    )
-    basis_half = new_basis.astype(jnp.bfloat16)
+    correlation = jnp.einsum("dk,dm->km", full_image[0], full_image[0], precision=highest)
+    basis_half, kept_tile = orthogonalize(
+        correlation, full_image[0], image[0], jnp.take(kept_counts, own_sectors)
+    )
+    basis_half = basis_half[None]
+    kept_tile = kept_tile[None]
     mapped = jnp.einsum(
         "lxy,lyk->lxk", blocks, basis_half, preferred_element_type=jnp.float32
     ).astype(jnp.bfloat16)

time: 402 us -> 263 us (0.65); the launches traced: 396 us -> 263 us
  other arithmetic: 128 us -> 5.15 us
  blocking collectives: 11.6 us -> 44.8 us
  Pallas kernels: 0 us -> 28.9 us
  waiting for transfers between devices: 146 us -> 120 us
  matrix products: 39.7 us -> 19 us
  local copies, waits for them, and re-layouts: 28.5 us -> 11 us
  starting transfers between devices: 33.2 us -> 27.6 us
    another operation x18 -> x0, other arithmetic: 120 us -> none  [the longest x14 78.9 us: body(): factor = jnp.linalg.cholesky(correlation)]
    all_to_all x0 -> x1, blocking collectives: none -> 33.2 us  [fetch_pieces(): lax.all_to_all(outgoing, 'op', split_axis=1, concat_axis=1, tiled=True)]
    pallas_call x0 -> x1, Pallas kernels: none -> 28.9 us  [orthogonalize(): pl.pallas_call(orthogonalize_kernel, out_shape=(jax.ShapeDtypeStruct(imag...]
    all_to_all x2 -> x1, waiting for transfers between devices: 43.8 us -> 18.2 us  [fetch_pieces(): lax.all_to_all(outgoing, 'op', split_axis=1, concat_axis=1, tiled=True)]
    another operation x13 -> x0, matrix products: 20.8 us -> none  [the longest x7 15.3 us: body(): lax.linalg.triangular_solve(factor, full_image, left_side=False, lower=Tr...]
    another operation x17 -> x1, local copies, waits for them, and re-layouts: 13.8 us -> 0.01 us
    all_to_all x2 -> x1, starting transfers between devices: 17.2 us -> 11.6 us  [fetch_pieces(): lax.all_to_all(outgoing, 'op', split_axis=1, concat_axis=1, tiled=True)]
  transfers between devices with their start and end apart: 5 -> 4, of which waited for: 5 -> 4; matrix products, arithmetic and copies ran while one was open for 2% -> 2% of each run, Pallas kernels for 0% -> 0%
where the time goes in v1:
time: 263 us
  waiting for transfers between devices  120 us (46%)
  blocking collectives  44.8 us (17%)
  Pallas kernels  28.9 us (11%)
  starting transfers between devices  27.6 us (10%)
  matrix products  19 us (7%)
  local copies, waits for them, and re-layouts  11 us (4%)
  between operations  5.79 us (2%)
  other arithmetic  5.15 us (2%)
    all_to_all x2, waiting for transfers between devices, from_everyone(): lax.all_to_all(jnp.broadcast_to(value[None], (size, *value.shape)), axis,...  54.2 us
    all_to_all x1, waiting for transfers between devices, summed_on_arrival(): tiles = lax.all_to_all(in_blocks(value, dim, size), axis, 0, 0, tiled=True)  48 us
    all_to_all x1, blocking collectives, fetch_pieces(): lax.all_to_all(outgoing, 'op', split_axis=1, concat_axis=1, tiled=True)  33.2 us
    pallas_call x1, Pallas kernels, orthogonalize(): pl.pallas_call(orthogonalize_kernel, out_shape=(jax.ShapeDtypeStruct(imag...  28.9 us
    all_to_all x1, waiting for transfers between devices, fetch_pieces(): lax.all_to_all(outgoing, 'op', split_axis=1, concat_axis=1, tiled=True)  18.2 us
    all_to_all x1, starting transfers between devices, fetch_pieces(): lax.all_to_all(outgoing, 'op', split_axis=1, concat_axis=1, tiled=True)  11.6 us
    all_to_all x1, blocking collectives, from_everyone(): lax.all_to_all(jnp.broadcast_to(value[None], (size, *value.shape)), axis,...  11.6 us
    all_to_all x2, starting transfers between devices, from_everyone(): lax.all_to_all(jnp.broadcast_to(value[None], (size, *value.shape)), axis,...  10.3 us
  transfers between devices with their start and end apart: 4, of which 4 were waited for; matrix products, arithmetic and copies ran while one was open for 2% of the time, Pallas kernels for 0%

profile of v1, /device:TPU:2, one launch (start us, length us, event | category | flops | bytes accessed | tf_op | source)
XLA Modules:
  0.0 262.6 jit_solution(8900170670336339168)
XLA Ops:
  0.6 1.6 broadcast_in_dim.147
  2.3 4.5 %all-to-all-start = ((bf16[8,1,16,1024]{3,2,1,0:T(8,128)(2,1)}), bf16[8,1,16,1024]{3,2,1,0:T(8,128)(2,1)S(1)}, u32[]{:S(2)}, u32[]{:S(2)}) async-start(bf16[8,1,16,1024]{3,2,1,0:T(8,128)(2,1)} %broadcast_in_dim.147), calls=%async_computation | async-start | bytes 524288 | tf_op jit(solution)/shard_map/all_to_all | solution.py:136
  7.5 6.8 %all-to-all-done = bf16[8,1,16,1024]{3,2,1,0:T(8,128)(2,1)S(1)} async-done(((bf16[8,1,16,1024]{3,2,1,0:T(8,128)(2,1)}), bf16[8,1,16,1024]{3,2,1,0:T(8,128)(2,1)S(1)}, u32[]{:S(2)}, u32[]{:S(2)}) %all-to-all-start) | async-done | bytes 262176 | tf_op jit(solution)/shard_map/all_to_all | solution.py:136
  14.9 1.1 bitcast_select_fusion.1
  16.1 11.6 %all-to-all-start.1 = ((bf16[1,32,16,1024]{3,2,0,1:T(8,128)(2,1)}), bf16[1,32,16,1024]{3,2,0,1:T(8,128)(2,1)S(1)}, u32[]{:S(2)}, u32[]{:S(2)}) async-start(bf16[1,32,16,1024]{3,2,0,1:T(8,128)(2,1)} %bitcast_select_fusion.1), calls=%async_computation.1 | async-start | bytes 2097152 | tf_op jit(solution)/shard_map/all_to_all | solution.py:172
  33.3 1.5 fusion.17
  34.8 2.4 fusion.21
  37.2 18.2 %all-to-all-done.1 = bf16[1,32,16,1024]{3,2,0,1:T(8,128)(2,1)S(1)} async-done(((bf16[1,32,16,1024]{3,2,0,1:T(8,128)(2,1)}), bf16[1,32,16,1024]{3,2,0,1:T(8,128)(2,1)S(1)}, u32[]{:S(2)}, u32[]{:S(2)}) %all-to-all-start.1) | async-done | bytes 1048608 | tf_op jit(solution)/shard_map/all_to_all | solution.py:172
  55.5 1.3 fusion.6
  58.4 3.3 %add_bitcast_fusion = f32[1024,1,512]{0,2,1:T(8,128)} fusion(f32[512,1024]{1,0:T(8,128)S(1)} %copy-done.1, f32[512,512]{1,0:T(8,128)S(1)} %fusion.15, bf16[512,1024]{1,0:T(8,128)(2,1)S(1)} %fusion.6, f32[]{:T(128)} %bitcast.6), kind=kOutput, calls=%fused_computation.8 | convolution fusion | flops 3222274048 | bytes 6291460 | tf_op jit(solution)/shard_map/lcr,lck->rlk/dot_general | solution.py:227
  61.6 2.9 %copy.16 = f32[1024,1,512]{2,0,1:T(8,128)} copy(f32[1024,1,512]{0,2,1:T(8,128)} %add_bitcast_fusion) | data formatting | bytes 4194304 | tf_op jit(solution)/shard_map/add | solution.py:225
  64.5 5.7 %all-to-all-start.2 = ((f32[32,32,1,512]{3,1,2,0:T(8,128)}), f32[32,32,1,512]{3,1,2,0:T(8,128)}, u32[]{:S(2)}, u32[]{:S(2)}) async-start(f32[32,32,1,512]{3,1,2,0:T(8,128)} %bitcast.70), calls=%async_computation.2 | async-start | bytes 4194304 | tf_op jit(solution)/shard_map/all_to_all | solution.py:159
  71.6 48.0 %all-to-all-done.2 = f32[32,32,1,512]{3,1,2,0:T(8,128)} async-done(((f32[32,32,1,512]{3,1,2,0:T(8,128)}), f32[32,32,1,512]{3,1,2,0:T(8,128)}, u32[]{:S(2)}, u32[]{:S(2)}) %all-to-all-start.2) | async-done | bytes 2097184 | tf_op jit(solution)/shard_map/all_to_all | solution.py:159
  119.5 1.7 reduce_sum.19
  121.4 1.6 broadcast_in_dim.151
  122.9 5.8 %all-to-all-start.3 = ((f32[32,1,32,512]{3,2,1,0:T(8,128)}), f32[32,1,32,512]{3,2,1,0:T(8,128)}, u32[]{:S(2)}, u32[]{:S(2)}) async-start(f32[32,1,32,512]{3,2,1,0:T(8,128)} %broadcast_in_dim.151), calls=%async_computation.3 | async-start | bytes 4194304 | tf_op jit(solution)/shard_map/all_to_all | solution.py:136
  128.8 47.4 %all-to-all-done.3 = f32[32,1,32,512]{3,2,1,0:T(8,128)} async-done(((f32[32,1,32,512]{3,2,1,0:T(8,128)}), f32[32,1,32,512]{3,2,1,0:T(8,128)}, u32[]{:S(2)}, u32[]{:S(2)}) %all-to-all-start.3) | async-done | bytes 2097184 | tf_op jit(solution)/shard_map/all_to_all | solution.py:136
  176.1 5.7 %fusion.12.corr_ref = f32[512,512]{1,0:T(8,128)S(1)} fusion(f32[32,1,32,512]{3,2,1,0:T(8,128)} %all-to-all-done.3), kind=kOutput, calls=%fused_computation.11 | convolution fusion | flops 3221225472 | bytes 3145728 | tf_op jit(solution)/shard_map/dk,dm->km/dot_general | solution.py:236
  181.8 28.9 %orthogonalize.1 = (bf16[1024,512]{1,0:T(8,128)(2,1)S(1)}, f32[32,512]{1,0:T(8,128)}) custom-call(s32[1]{0:T(128)} %select_n.180.kept_ref, f32[512,512]{1,0:T(8,128)S(1)} %fusion.12.corr_ref, f32[1024,512]{1,0:T(8,128)} %bitcast.25.image_ref, f32[32,512]{1,0:T(8,128)S(1)} %and_select_fusion.tile_ref), custom_call_target="tpu_custom_call" | custom-call | tf_op jit(solution)/shard_map/orthogonalize/pallas_call | solution.py:116
  210.8 11.6 %all_to_all.30 = bf16[8,1,32,512]{3,2,1,0:T(8,128)(2,1)S(1)} all-to-all(bf16[8,1,32,512]{3,2,1,0:T(8,128)(2,1)S(1)} %broadcast_in_dim.154), channel_id=1, replica_groups=mesh['sec'=8,'op'=32] {'sec'}, dimensions={0} | all-to-all | bytes 524288 | tf_op jit(solution)/shard_map/all_to_all | solution.py:136
  222.4 1.6 gather_fusion.1
  224.0 1.4 bitcast_select_fusion
  225.3 33.2 %all_to_all.31 = bf16[1,32,32,512]{3,2,0,1:T(8,128)(2,1)} all-to-all(bf16[1,32,32,512]{3,2,0,1:T(8,128)(2,1)S(1)} %bitcast_select_fusion), channel_id=1, replica_groups=mesh['sec'=8,'op'=32] {'op'}, dimensions={1} | all-to-all | bytes 2097152 | tf_op jit(solution)/shard_map/all_to_all | solution.py:172
  258.5 4.0 %convolution_bitcast_fusion = f32[1,1,512,512]{3,2,1,0:T(8,128)} fusion(bf16[1024,512]{1,0:T(8,128)(2,1)} %bitcast.73, bf16[1024,512]{1,0:T(8,128)(2,1)S(1)} %get-tuple-element.5, bf16[1,1,1024,1024]{3,2,1,0:T(8,128)(2,1)S(1)} %copy-done), kind=kOutput, calls=%fused_computation.12 | convolution fusion | flops 1611137024 | bytes 5242880 | tf_op jit(solution)/shard_map/lxk,lxm->lkm/dot_general | solution.py:247
  (29 shorter events, 5.0 us)
Async XLA Ops:
  0.6 54.8 %copy-start = (bf16[1,1,1024,1024]{3,2,1,0:T(8,128)(2,1)S(1)}, bf16[1,1,1024,1024]{3,2,1,0:T(8,128)(2,1)}, u32[]{:S(2)}) copy-start(bf16[1,1,1024,1024]{3,2,1,0:T(8,128)(2,1)} %param.9) | copy-start | bytes 6291460
  2.3 12.0 %all-to-all-start = ((bf16[8,1,16,1024]{3,2,1,0:T(8,128)(2,1)}), bf16[8,1,16,1024]{3,2,1,0:T(8,128)(2,1)S(1)}, u32[]{:S(2)}, u32[]{:S(2)}) async-start(bf16[8,1,16,1024]{3,2,1,0:T(8,128)(2,1)} %broadcast_in_dim.147), calls=%async_computation | async-start | bytes 524288 | tf_op jit(solution)/shard_map/all_to_all | solution.py:136
  14.9 16.4 %copy-start.3 = (s32[8]{0:T(128)S(1)}, s32[8]{0:T(128)}, u32[]{:S(2)}) copy-start(s32[8]{0:T(128)} %param.11) | copy-start | bytes 100
  14.9 18.3 %copy-start.2 = (bf16[1,16,1024]{2,1,0:T(8,128)(2,1)S(1)}, bf16[1,16,1024]{2,1,0:T(8,128)(2,1)}, u32[]{:S(2)}) copy-start(bf16[1,16,1024]{2,1,0:T(8,128)(2,1)} %param.8) | copy-start | bytes 98308
  16.1 39.3 %all-to-all-start.1 = ((bf16[1,32,16,1024]{3,2,0,1:T(8,128)(2,1)}), bf16[1,32,16,1024]{3,2,0,1:T(8,128)(2,1)S(1)}, u32[]{:S(2)}, u32[]{:S(2)}) async-start(bf16[1,32,16,1024]{3,2,0,1:T(8,128)(2,1)} %bitcast_select_fusion.1), calls=%async_computation.1 | async-start | bytes 2097152 | tf_op jit(solution)/shard_map/all_to_all | solution.py:172
  55.5 1.3 copy-start.4
  56.8 1.6 copy-start.1
  64.5 5.8 %copy-start.5 = (s32[8]{0:T(128)S(1)}, s32[8]{0:T(128)}, u32[]{:S(2)}) copy-start(s32[8]{0:T(128)} %param.12) | copy-start | bytes 100
  64.5 55.0 %all-to-all-start.2 = ((f32[32,32,1,512]{3,1,2,0:T(8,128)}), f32[32,32,1,512]{3,1,2,0:T(8,128)}, u32[]{:S(2)}, u32[]{:S(2)}) async-start(f32[32,32,1,512]{3,1,2,0:T(8,128)} %bitcast.70), calls=%async_computation.2 | async-start | bytes 4194304 | tf_op jit(solution)/shard_map/all_to_all | solution.py:159
  122.9 53.2 %all-to-all-start.3 = ((f32[32,1,32,512]{3,2,1,0:T(8,128)}), f32[32,1,32,512]{3,2,1,0:T(8,128)}, u32[]{:S(2)}, u32[]{:S(2)}) async-start(f32[32,1,32,512]{3,2,1,0:T(8,128)} %broadcast_in_dim.151), calls=%async_computation.3 | async-start | bytes 4194304 | tf_op jit(solution)/shard_map/all_to_all | solution.py:136

commit v2 on v1

v2 whole, which is shorter than its diff:
```python
import jax
import jax.numpy as jnp
from jax import lax
from jax.experimental import pallas as pl
from jax.experimental.pallas import tpu as pltpu
from jax.sharding import PartitionSpec as P

HIGHEST = lax.Precision.HIGHEST
LANE = 128
CUTS = (0, 512)


def dot(a, b, ca, cb):
    return lax.dot_general(
        a, b, (((ca,), (cb,)), ((), ())), precision=HIGHEST, preferred_element_type=jnp.float32
    )


def factor_block(block):
    n = LANE
    sub = lax.broadcasted_iota(jnp.int32, (8, LANE), 0)
    lane = lax.broadcasted_iota(jnp.int32, (8, LANE), 1)
    groups = n // 8
    per = 4
    rows = [block[8 * g:8 * g + 8, :] for g in range(groups)]
    aug = [jnp.where(lane == sub + 8 * g, 1.0, 0.0).astype(jnp.float32) for g in range(groups)]
    out = []
    for s in range(0, groups, per):
        done_r, done_w = [], []
        for g in range(s, s + per):
            v, w = rows[g], aug[g]
            cols = [jnp.broadcast_to(v[:, 8 * g + j:8 * g + j + 1], (8, LANE)) for j in range(8)]
            e = {(i, j): jnp.broadcast_to(cols[j][i:i + 1, :], (8, LANE)) for j in range(8) for i in range(j, 8)}
            inv, low = [], {}
            for j in range(8):
                d = e[j, j]
                r = lax.rsqrt(d)
                r = r * (1.5 - 0.5 * d * r * r)
                inv.append(r)
                for i in range(j + 1, 8):
                    low[i, j] = e[i, j] * r
                for k in range(j + 1, 8):
                    for i in range(k, 8):
                        e[i, k] = e[i, k] - low[i, j] * low[k, j]
            m = {}
            for c in range(8):
                m[c, c] = inv[c]
                for i in range(c + 1, 8):
                    t = low[i, c] * m[c, c]
                    for k in range(c + 1, i):
                        t = t + low[i, k] * m[k, c]
                    m[i, c] = -t * inv[i]
            rv = rw = None
            mcols = []
            for j in range(8):
                mc = jnp.zeros((8, LANE), jnp.float32)
                for i in range(j, 8):
                    mc = jnp.where(sub == i, m[i, j], mc)
                tv = mc * jnp.broadcast_to(v[j:j + 1, :], (8, LANE))
                tw = mc * jnp.broadcast_to(w[j:j + 1, :], (8, LANE))
                rv = tv if rv is None else rv + tv
                rw = tw if rw is None else rw + tw
            out.append(rw)
            done_r.append(rv)
            done_w.append(rw)
            if g + 1 < s + per:
                rvb = [jnp.broadcast_to(rv[j:j + 1, :], (8, LANE)) for j in range(8)]
                rwb = [jnp.broadcast_to(rw[j:j + 1, :], (8, LANE)) for j in range(8)]
                for h in range(g + 1, s + per):
                    raw = [jnp.broadcast_to(rows[h][:, 8 * g + j:8 * g + j + 1], (8, LANE)) for j in range(8)]
                    nv, nw = rows[h], aug[h]
                    for i in range(8):
                        f = raw[0] * m[i, 0]
                        for k in range(1, i + 1):
                            f = f + raw[k] * m[i, k]
                        nv = nv - f * rvb[i]
                        nw = nw - f * rwb[i]
                    rows[h], aug[h] = nv, nw
        if s + per < groups:
            left = jnp.concatenate(done_r, axis=0)
            both = jnp.concatenate([left, jnp.concatenate(done_w, axis=0)], axis=1)
            rest = 8 * (s + per)
            delta = dot(left, both, 0, 0)
            for h in range(s + per, groups):
                rows[h] = rows[h] - delta[8 * h:8 * h + 8, :LANE]
                aug[h] = aug[h] - delta[8 * h:8 * h + 8, LANE:]
    return jnp.concatenate(out, axis=0)


def basis_kernel(offset, scalars_ref, image_ref, *refs):
    count = len(refs) - 6
    before = refs[:count]
    half_ref, tile_half_ref, kept_ref, q_ref, a_ref, t_ref = refs[count:]
    rows, width = image_ref.shape
    kept, own = scalars_ref[0], scalars_ref[1]
    if before:
        t_ref[...] = image_ref[...]
        for earlier in before:
            t_ref[...] = t_ref[...] - dot(
                earlier[...], dot(earlier[...], image_ref[...], 0, 0), 1, 0
            )
    else:
        t_ref[...] = image_ref[...]
    r_i = lax.broadcasted_iota(jnp.int32, (width, width), 0)
    c_i = lax.broadcasted_iota(jnp.int32, (width, width), 1)
    a_ref[...] = dot(t_ref[...], t_ref[...], 0, 0) + jnp.where(
        (r_i == c_i) & (c_i + offset >= kept), 1.0, 0.0
    )
    for lo in range(0, width, LANE):
        hi = lo + LANE
        inv = factor_block(a_ref[lo:hi, lo:hi])
        t = t_ref[:, lo:hi]
        if lo:
            t = t - dot(q_ref[:, :lo], a_ref[:lo, lo:hi], 1, 0)
        q = dot(t, inv, 1, 1)
        q_ref[:, lo:hi] = q
        half_ref[:, lo:hi] = q.astype(jnp.bfloat16)
        if hi < width:
            r = dot(inv, a_ref[lo:hi, hi:], 1, 0)
            a_ref[lo:hi, hi:] = r
            for c in range(hi, width, LANE):
                a_ref[c : c + LANE, c:] = a_ref[c : c + LANE, c:] - dot(
                    r[:, c - hi : c - hi + LANE], r[:, c - hi :], 0, 0
                )
    tile = kept_ref.shape[0]
    mine = q_ref[pl.ds(pl.multiple_of(own * tile, tile), tile), :]
    tile_half_ref[...] = mine.astype(jnp.bfloat16)
    kept_ref[...] = mine * float(rows) ** 0.5


def orthonormal(image, before, offset, scalars, tile):
    rows, width = image.shape
    vmem = pl.BlockSpec(memory_space=pltpu.VMEM)
    return pl.pallas_call(
        lambda *refs: basis_kernel(offset, *refs),
        out_shape=(
            jax.ShapeDtypeStruct((rows, width), jnp.bfloat16),
            jax.ShapeDtypeStruct((tile, width), jnp.bfloat16),
            jax.ShapeDtypeStruct((tile, width), jnp.float32),
            jax.ShapeDtypeStruct((rows, width), jnp.float32),
        ),
        in_specs=[pl.BlockSpec(memory_space=pltpu.SMEM)] + [vmem] * (1 + len(before)),
        out_specs=(vmem,) * 4,
        scratch_shapes=[
            pltpu.VMEM((width, width), jnp.float32),
            pltpu.VMEM((rows, width), jnp.float32),
        ],
        compiler_params=pltpu.CompilerParams(vmem_limit_bytes=40 << 20),
        cost_estimate=pl.CostEstimate(
            flops=40_000_000_000 * width // 512, bytes_accessed=rows * width * 12, transcendentals=0
        ),
        name="basis_%d" % offset,
    )(scalars, image, *before)


def from_everyone(value, axis):
    size = lax.axis_size(axis)
    return lax.all_to_all(
        jnp.broadcast_to(value[None], (size, *value.shape)), axis, 0, 0, tiled=True
    )


def source_sectors(target_map):
    sectors = jnp.arange(target_map.shape[1], dtype=jnp.int32)
    matches = target_map[:, :, None] == sectors[None, None, :]
    return jnp.sum(jnp.where(matches, sectors[None, :, None], 0), axis=1)


def fetch_pieces(own_slice, wanted_all):
    everyone = from_everyone(own_slice, "sec")
    outgoing = jnp.take(everyone, wanted_all, axis=0)
    incoming = lax.all_to_all(outgoing, "op", 0, 0, tiled=True)
    return incoming.reshape(-1, incoming.shape[-1])


def body(
    wavefunction,
    op_blocks,
    basis_guess,
    sector_sizes,
    kept_counts,
    target_map,
    noise_numerator,
    noise_denominator,
):
    state_count = wavefunction.shape[2]
    kept_width = basis_guess.shape[2]
    ops = lax.axis_size("op")
    tile_rows = state_count // ops
    sec_index = lax.axis_index("sec")
    op_index = lax.axis_index("op")
    noise_weight = noise_numerator[0].astype(jnp.float32) / noise_denominator[0].astype(jnp.float32)
    sources = source_sectors(target_map)
    wanted_all = jnp.take(sources, sec_index, axis=1)
    wanted = jnp.take(wanted_all, op_index)
    states = jnp.arange(state_count, dtype=jnp.int32)
    own_size = jnp.take(sector_sizes, sec_index)
    own_kept = jnp.take(kept_counts, sec_index)
    own_mask = states < own_size
    source_mask = states < jnp.take(sector_sizes, wanted)
    zero_half = jnp.zeros((), jnp.bfloat16)
    own_rows = jnp.where(own_mask[None, :], wavefunction[0], zero_half)
    moved = fetch_pieces(wavefunction[0], wanted_all)
    moved = jnp.where(source_mask[None, :], moved, zero_half)
    blocks = op_blocks[0, 0]
    perturbed = jnp.dot(moved, blocks, preferred_element_type=jnp.float32).astype(jnp.bfloat16)
    guess_rows = jnp.where(own_mask[:, None], basis_guess[0], zero_half)
    left = jnp.concatenate([perturbed, own_rows], axis=0)
    proj = jnp.dot(left, guess_rows, preferred_element_type=jnp.float32)
    is_noise = jnp.arange(left.shape[0]) < perturbed.shape[0]
    proj = proj * jnp.where(is_noise, noise_weight, jnp.float32(1.0))[:, None]
    proj_high = proj.astype(jnp.bfloat16)
    proj_low = (proj - proj_high.astype(jnp.float32)).astype(jnp.bfloat16)
    scalars = jnp.stack([own_kept, op_index])
    row_ids = op_index * tile_rows + jnp.arange(tile_rows, dtype=jnp.int32)
    row_mask = row_ids < own_size
    col_mask = jnp.arange(kept_width, dtype=jnp.int32) < own_kept
    cuts = list(zip(CUTS[:-1], CUTS[1:]))
    images = []
    sums = []
    for lo, hi in cuts:
        part = lax.dot_general(
            jnp.concatenate([left, left], axis=0),
            jnp.concatenate([proj_high[:, lo:hi], proj_low[:, lo:hi]], axis=0),
            (((0,), (0,)), ((), ())),
            preferred_element_type=jnp.float32,
        ).astype(jnp.bfloat16)
        tiles = lax.all_to_all(part.reshape(ops, tile_rows, hi - lo), "op", 0, 0, tiled=True)
        sums.append(jnp.sum(tiles.astype(jnp.float32), axis=0))
    for (lo, hi), total in zip(cuts, sums):
        image = jnp.where(row_mask[:, None] & col_mask[None, lo:hi], total, jnp.float32(0.0))
        images.append(from_everyone(image, "op").reshape(state_count, hi - lo))
    before, kept_tiles, mapped, fetched = [], [], [], []
    for (lo, hi), image in zip(cuts, images):
        half, tile_half, kept_tile, q = orthonormal(image, before, lo, scalars, tile_rows)
        before.append(q)
        kept_tiles.append(kept_tile)
        fetched.append(fetch_pieces(tile_half, wanted_all))
        mapped.append(
            jnp.dot(blocks, half, preferred_element_type=jnp.float32).astype(jnp.bfloat16)
        )
    mapped = jnp.concatenate(mapped, axis=1)
    rotated = jnp.concatenate(
        [
            lax.dot_general(
                source, mapped, (((0,), (0,)), ((), ())), preferred_element_type=jnp.float32
            )
            for source in fetched
        ],
        axis=0,
    )
    return (jnp.concatenate(kept_tiles, axis=1)[None], rotated[None, None])


def solution(mesh):
    placed = (
        P("sec", "op", None),
        P("op", "sec", None, None),
        P("sec", None, None),
        P(),
        P(),
        P(),
        P(),
        P(),
    )
    return jax.shard_map(
        body,
        mesh=mesh,
        in_specs=placed,
        out_specs=(P("sec", "op", None), P("op", "sec", None, None)),
        check_vma=False,
    )
```

time: 263 us -> 232 us (0.88)
  waiting for transfers between devices: 120 us -> 104 us
  matrix products: 19 us -> 8.65 us
  local copies, waits for them, and re-layouts: 11 us -> 7.35 us
  Pallas kernels: 28.9 us -> 31.8 us
    all_to_all x2, waiting for transfers between devices: 66.2 us -> 48.6 us  [the longest x1 25.4 us: body(): lax.all_to_all(part.reshape(ops, tile_rows, hi - lo), 'op', 0, 0, tiled=T...]
    dot_general x7 -> x4, matrix products: 19 us -> 8.65 us  [the longest x1 4.04 us: body(): lax.dot_general(source, mapped, (((0,), (0,)), ((), ())), preferred_eleme...]
    add x1 -> x0, local copies, waits for them, and re-layouts: 2.91 us -> none  [body(): contribution + noise_weight * jnp.einsum('lcr,lck->rlk', perturbed_part,...]
    pallas_call x1, Pallas kernels: 28.9 us -> 31.8 us  [orthonormal(): pl.pallas_call(lambda *refs: basis_kernel(offset, *refs), out_shape=(jax....]
  transfers between devices with their start and end apart: 4 -> 4, of which waited for: 4 -> 4; matrix products, arithmetic and copies ran while one was open for 2% -> 1% of each run, Pallas kernels for 0% -> 0%
where the time goes in v2:
time: 232 us; the launch traced here: 231 us
  waiting for transfers between devices  104 us (45%)
  blocking collectives  43.5 us (19%)
  Pallas kernels  31.8 us (14%)
  starting transfers between devices  27.6 us (12%)
  matrix products  8.65 us (4%)
  local copies, waits for them, and re-layouts  7.35 us (3%)
  between operations  4.66 us (2%)
  other arithmetic  3.67 us (2%)
    all_to_all x2, waiting for transfers between devices, from_everyone(): lax.all_to_all(jnp.broadcast_to(value[None], (size, *value.shape)), axis,...  55.5 us
    all_to_all x1, blocking collectives, fetch_pieces(): incoming = lax.all_to_all(outgoing, 'op', 0, 0, tiled=True)  33.2 us
    pallas_call x1, Pallas kernels, orthonormal(): pl.pallas_call(lambda *refs: basis_kernel(offset, *refs), out_shape=(jax....  31.8 us
    all_to_all x1, waiting for transfers between devices, body(): lax.all_to_all(part.reshape(ops, tile_rows, hi - lo), 'op', 0, 0, tiled=T...  25.4 us
    all_to_all x1, waiting for transfers between devices, fetch_pieces(): incoming = lax.all_to_all(outgoing, 'op', 0, 0, tiled=True)  23.2 us
    all_to_all x1, starting transfers between devices, fetch_pieces(): incoming = lax.all_to_all(outgoing, 'op', 0, 0, tiled=True)  11.6 us
    all_to_all x1, blocking collectives, from_everyone(): lax.all_to_all(jnp.broadcast_to(value[None], (size, *value.shape)), axis,...  10.3 us
    all_to_all x2, starting transfers between devices, from_everyone(): lax.all_to_all(jnp.broadcast_to(value[None], (size, *value.shape)), axis,...  10.3 us
  transfers between devices with their start and end apart: 4, of which 4 were waited for; matrix products, arithmetic and copies ran while one was open for 1% of the time, Pallas kernels for 0%

profile of v2, /device:TPU:2, one launch (start us, length us, event | category | flops | bytes accessed | tf_op | source)
XLA Modules:
  0.0 231.3 jit_solution(9947167482782894083)
XLA Ops:
  0.6 1.6 broadcast_in_dim.146
  2.3 4.5 %all-to-all-start = ((bf16[8,16,1024]{2,1,0:T(8,128)(2,1)}), bf16[8,16,1024]{2,1,0:T(8,128)(2,1)S(1)}, u32[]{:S(2)}, u32[]{:S(2)}) async-start(bf16[8,16,1024]{2,1,0:T(8,128)(2,1)} %broadcast_in_dim.146), calls=%async_computation | async-start | bytes 524288 | tf_op jit(solution)/shard_map/all_to_all | solution.py:158
  6.8 0.7 select_reduce_fusion
  7.5 6.8 %all-to-all-done = bf16[8,16,1024]{2,1,0:T(8,128)(2,1)S(1)} async-done(((bf16[8,16,1024]{2,1,0:T(8,128)(2,1)}), bf16[8,16,1024]{2,1,0:T(8,128)(2,1)S(1)}, u32[]{:S(2)}, u32[]{:S(2)}) %all-to-all-start) | async-done | bytes 262176 | tf_op jit(solution)/shard_map/all_to_all | solution.py:158
  14.3 0.6 gather_fusion
  14.9 1.1 broadcast_select_fusion.1
  16.1 11.6 %all-to-all-start.1 = ((bf16[32,16,1024]{2,1,0:T(8,128)(2,1)}), bf16[32,16,1024]{2,1,0:T(8,128)(2,1)S(1)}, u32[]{:S(2)}, u32[]{:S(2)}) async-start(bf16[32,16,1024]{2,1,0:T(8,128)(2,1)} %broadcast_select_fusion.1), calls=%async_computation.1 | async-start | bytes 2097152 | tf_op jit(solution)/shard_map/all_to_all | solution.py:172
  30.3 0.6 fusion.36
  32.2 23.2 %all-to-all-done.1 = bf16[32,16,1024]{2,1,0:T(8,128)(2,1)S(1)} async-done(((bf16[32,16,1024]{2,1,0:T(8,128)(2,1)}), bf16[32,16,1024]{2,1,0:T(8,128)(2,1)S(1)}, u32[]{:S(2)}, u32[]{:S(2)}) %all-to-all-start.1) | async-done | bytes 1048608 | tf_op jit(solution)/shard_map/all_to_all | solution.py:172
  55.5 1.3 fusion.12
  56.8 0.8 subtract_convert_fusion
  57.6 2.5 %fusion.18 = bf16[1024,512]{1,0:T(8,128)(2,1)} fusion(bf16[16,1024]{1,0:T(8,128)(2,1)S(1)} %broadcast_select_fusion.3, bf16[512,1024]{1,0:T(8,128)(2,1)S(1)} %fusion.12, bf16[528,512]{1,0:T(8,128)(2,1)S(1)} %get-tuple-element.63, bf16[528,512]{1,0:T(8,128)(2,1)S(1)} %get-tuple-element.64), kind=kOutput, calls=%fused_computation.17 | convolution fusion | flops 1118633984 | bytes 3211264 | tf_op jit(solution)/shard_map/dot_general | solution.py:222
  60.1 5.7 %all-to-all-start.2 = ((bf16[32,32,512]{2,1,0:T(8,128)(2,1)}), bf16[32,32,512]{2,1,0:T(8,128)(2,1)S(1)}, u32[]{:S(2)}, u32[]{:S(2)}) async-start(bf16[32,32,512]{2,1,0:T(8,128)(2,1)} %bitcast.42), calls=%async_computation.2 | async-start | bytes 2097152 | tf_op jit(solution)/shard_map/all_to_all | solution.py:228
  65.8 0.7 dynamic-slice.11
  67.2 25.4 %all-to-all-done.2 = bf16[32,32,512]{2,1,0:T(8,128)(2,1)S(1)} async-done(((bf16[32,32,512]{2,1,0:T(8,128)(2,1)}), bf16[32,32,512]{2,1,0:T(8,128)(2,1)S(1)}, u32[]{:S(2)}, u32[]{:S(2)}) %all-to-all-start.2) | async-done | bytes 1048608 | tf_op jit(solution)/shard_map/all_to_all | solution.py:228
  92.8 1.6 broadcast_in_dim.156
  94.4 5.8 %all-to-all-start.3 = ((f32[32,32,512]{2,1,0:T(8,128)}), f32[32,32,512]{2,1,0:T(8,128)}, u32[]{:S(2)}, u32[]{:S(2)}) async-start(f32[32,32,512]{2,1,0:T(8,128)} %broadcast_in_dim.156), calls=%async_computation.3 | async-start | bytes 4194304 | tf_op jit(solution)/shard_map/all_to_all | solution.py:158
  100.3 48.7 %all-to-all-done.3 = f32[32,32,512]{2,1,0:T(8,128)} async-done(((f32[32,32,512]{2,1,0:T(8,128)}), f32[32,32,512]{2,1,0:T(8,128)}, u32[]{:S(2)}, u32[]{:S(2)}) %all-to-all-start.3) | async-done | bytes 2097184 | tf_op jit(solution)/shard_map/all_to_all | solution.py:158
  149.0 31.8 %basis_0.1 = (bf16[1024,512]{1,0:T(8,128)(2,1)S(1)}, bf16[32,512]{1,0:T(8,128)(2,1)S(1)}, f32[32,512]{1,0:T(8,128)}, f32[1024,512]{1,0:T(8,128)}) custom-call(s32[2]{0:T(128)S(1)} %pad_add_fusion.refs_0_, f32[1024,512]{1,0:T(8,128)} %bitcast.17.refs_1_), custom_call_target="tpu_custom_call" | custom-call | flops 40000000000 | bytes 6291456 | tf_op jit(solution)/shard_map/basis_0/pallas_call | solution.py:134
  180.8 10.3 %all_to_all.30 = bf16[8,32,512]{2,1,0:T(8,128)(2,1)S(1)} all-to-all(bf16[8,32,512]{2,1,0:T(8,128)(2,1)S(1)} %broadcast_in_dim.159), channel_id=1, replica_groups=mesh['sec'=8,'op'=32] {'sec'}, dimensions={0} | all-to-all | bytes 524288 | tf_op jit(solution)/shard_map/all_to_all | solution.py:158
  191.1 1.6 gather_fusion.1
  192.7 1.4 broadcast_select_fusion
  194.1 33.2 %all_to_all.31 = bf16[32,32,512]{2,1,0:T(8,128)(2,1)} all-to-all(bf16[32,32,512]{2,1,0:T(8,128)(2,1)S(1)} %broadcast_select_fusion), channel_id=1, replica_groups=mesh['sec'=8,'op'=32] {'op'}, dimensions={0} | all-to-all | bytes 2097152 | tf_op jit(solution)/shard_map/all_to_all | solution.py:172
  227.2 4.0 %convolution_bitcast_fusion = f32[1,1,512,512]{3,2,1,0:T(8,128)} fusion(bf16[1024,512]{1,0:T(8,128)(2,1)} %bitcast.43, bf16[1024,512]{1,0:T(8,128)(2,1)S(1)} %get-tuple-element.7, bf16[1,1,1024,1024]{3,2,1,0:T(8,128)(2,1)S(1)} %copy-done), kind=kOutput, calls=%fused_computation.19 | convolution fusion | flops 1611137024 | bytes 5242880 | tf_op jit(solution)/shard_map/dot_general | solution.py:245
  (25 shorter events, 1.1 us)
Async XLA Ops:
  0.6 54.8 %copy-start = (bf16[1,1,1024,1024]{3,2,1,0:T(8,128)(2,1)S(1)}, bf16[1,1,1024,1024]{3,2,1,0:T(8,128)(2,1)}, u32[]{:S(2)}) copy-start(bf16[1,1,1024,1024]{3,2,1,0:T(8,128)(2,1)} %param.9) | copy-start | bytes 6291460
  2.3 12.0 %all-to-all-start = ((bf16[8,16,1024]{2,1,0:T(8,128)(2,1)}), bf16[8,16,1024]{2,1,0:T(8,128)(2,1)S(1)}, u32[]{:S(2)}, u32[]{:S(2)}) async-start(bf16[8,16,1024]{2,1,0:T(8,128)(2,1)} %broadcast_in_dim.146), calls=%async_computation | async-start | bytes 524288 | tf_op jit(solution)/shard_map/all_to_all | solution.py:158
  14.9 15.4 %copy-start.2 = (s32[8]{0:T(128)S(1)}, s32[8]{0:T(128)}, u32[]{:S(2)}) copy-start(s32[8]{0:T(128)} %param.11) | copy-start | bytes 100
  14.9 17.2 %copy-start.1 = (bf16[1,16,1024]{2,1,0:T(8,128)(2,1)S(1)}, bf16[1,16,1024]{2,1,0:T(8,128)(2,1)}, u32[]{:S(2)}) copy-start(bf16[1,16,1024]{2,1,0:T(8,128)(2,1)} %param.8) | copy-start | bytes 98308
  16.1 39.3 %all-to-all-start.1 = ((bf16[32,16,1024]{2,1,0:T(8,128)(2,1)}), bf16[32,16,1024]{2,1,0:T(8,128)(2,1)S(1)}, u32[]{:S(2)}, u32[]{:S(2)}) async-start(bf16[32,16,1024]{2,1,0:T(8,128)(2,1)} %broadcast_select_fusion.1), calls=%async_computation.1 | async-start | bytes 2097152 | tf_op jit(solution)/shard_map/all_to_all | solution.py:172
  55.5 1.3 copy-start.3
  60.1 5.7 %copy-start.4 = (s32[8]{0:T(128)S(1)}, s32[8]{0:T(128)}, u32[]{:S(2)}) copy-start(s32[8]{0:T(128)} %param.12) | copy-start | bytes 100
  60.1 32.4 %all-to-all-start.2 = ((bf16[32,32,512]{2,1,0:T(8,128)(2,1)}), bf16[32,32,512]{2,1,0:T(8,128)(2,1)S(1)}, u32[]{:S(2)}, u32[]{:S(2)}) async-start(bf16[32,32,512]{2,1,0:T(8,128)(2,1)} %bitcast.42), calls=%async_computation.2 | async-start | bytes 2097152 | tf_op jit(solution)/shard_map/all_to_all | solution.py:228
  94.4 54.6 %all-to-all-start.3 = ((f32[32,32,512]{2,1,0:T(8,128)}), f32[32,32,512]{2,1,0:T(8,128)}, u32[]{:S(2)}, u32[]{:S(2)}) async-start(f32[32,32,512]{2,1,0:T(8,128)} %broadcast_in_dim.156), calls=%async_computation.3 | async-start | bytes 4194304 | tf_op jit(solution)/shard_map/all_to_all | solution.py:158

commit v3 on v2

--- a/solution.py
+++ b/solution.py
@@ -166,11 +166,40 @@
     return jnp.sum(jnp.where(matches, sectors[None, :, None], 0), axis=1)
 
 
-def fetch_pieces(own_slice, wanted_all):
-    everyone = from_everyone(own_slice, "sec")
-    outgoing = jnp.take(everyone, wanted_all, axis=0)
+def gather_sectors(value):
+    size = lax.axis_size("sec")
+    other = lax.ppermute(value, "sec", [(i, i ^ 1) for i in range(size)])
+    pair = jnp.stack([value, other])
+    pairs = [pair] + [
+        lax.ppermute(pair, "sec", [(i, (i + 2 * step) % size) for i in range(size)])
+        for step in range(1, size // 2)
+    ]
+    return jnp.concatenate(pairs, axis=0)
+
+
+def place_of(sector, own):
+    chips = lax.axis_size("sec") // 2
+    return (own // 2 - sector // 2 + chips) % chips * 2 + (own + sector) % 2
+
+
+def fetch_pieces(own_slice, places):
+    outgoing = jnp.take(gather_sectors(own_slice), places, axis=0, mode="clip")
     incoming = lax.all_to_all(outgoing, "op", 0, 0, tiled=True)
     return incoming.reshape(-1, incoming.shape[-1])
+
+
+def in_halves(value):
+    high = value.astype(jnp.bfloat16)
+    return high, (value - high.astype(jnp.float32)).astype(jnp.bfloat16)
+
+
+def from_left(left, high, low):
+    return lax.dot_general(
+        jnp.concatenate([left, left], axis=0),
+        jnp.concatenate([high, low], axis=0),
+        (((0,), (0,)), ((), ())),
+        preferred_element_type=jnp.float32,
+    )
 
 
 def body(
@@ -193,24 +222,27 @@
     sources = source_sectors(target_map)
     wanted_all = jnp.take(sources, sec_index, axis=1)
     wanted = jnp.take(wanted_all, op_index)
+    places = place_of(wanted_all, sec_index)
     states = jnp.arange(state_count, dtype=jnp.int32)
     own_size = jnp.take(sector_sizes, sec_index)
     own_kept = jnp.take(kept_counts, sec_index)
     own_mask = states < own_size
     source_mask = states < jnp.take(sector_sizes, wanted)
     zero_half = jnp.zeros((), jnp.bfloat16)
-    own_rows = jnp.where(own_mask[None, :], wavefunction[0], zero_half)
-    moved = fetch_pieces(wavefunction[0], wanted_all)
+    own_all = lax.all_gather(wavefunction[0], "op", axis=0, tiled=True)
+    moved = fetch_pieces(wavefunction[0], places)
     moved = jnp.where(source_mask[None, :], moved, zero_half)
     blocks = op_blocks[0, 0]
     perturbed = jnp.dot(moved, blocks, preferred_element_type=jnp.float32).astype(jnp.bfloat16)
     guess_rows = jnp.where(own_mask[:, None], basis_guess[0], zero_half)
-    left = jnp.concatenate([perturbed, own_rows], axis=0)
-    proj = jnp.dot(left, guess_rows, preferred_element_type=jnp.float32)
-    is_noise = jnp.arange(left.shape[0]) < perturbed.shape[0]
-    proj = proj * jnp.where(is_noise, noise_weight, jnp.float32(1.0))[:, None]
-    proj_high = proj.astype(jnp.bfloat16)
-    proj_low = (proj - proj_high.astype(jnp.float32)).astype(jnp.bfloat16)
+    proj = noise_weight * jnp.dot(perturbed, guess_rows, preferred_element_type=jnp.float32)
+    proj_high, proj_low = in_halves(proj)
+    own_all = jnp.where(own_mask[None, :], own_all, zero_half)
+    own_columns = lax.dynamic_slice_in_dim(own_all, op_index * tile_rows, tile_rows, 1)
+    own_high, own_low = in_halves(
+        jnp.dot(own_all, guess_rows, preferred_element_type=jnp.float32)
+    )
+    own_image = from_left(own_columns, own_high, own_low)
     scalars = jnp.stack([own_kept, op_index])
     row_ids = op_index * tile_rows + jnp.arange(tile_rows, dtype=jnp.int32)
     row_mask = row_ids < own_size
@@ -219,14 +251,9 @@
     images = []
     sums = []
     for lo, hi in cuts:
-        part = lax.dot_general(
-            jnp.concatenate([left, left], axis=0),
-            jnp.concatenate([proj_high[:, lo:hi], proj_low[:, lo:hi]], axis=0),
-            (((0,), (0,)), ((), ())),
-            preferred_element_type=jnp.float32,
-        ).astype(jnp.bfloat16)
+        part = from_left(perturbed, proj_high[:, lo:hi], proj_low[:, lo:hi]).astype(jnp.bfloat16)
         tiles = lax.all_to_all(part.reshape(ops, tile_rows, hi - lo), "op", 0, 0, tiled=True)
-        sums.append(jnp.sum(tiles.astype(jnp.float32), axis=0))
+        sums.append(jnp.sum(tiles.astype(jnp.float32), axis=0) + own_image[:, lo:hi])
     for (lo, hi), total in zip(cuts, sums):
         image = jnp.where(row_mask[:, None] & col_mask[None, lo:hi], total, jnp.float32(0.0))
         images.append(from_everyone(image, "op").reshape(state_count, hi - lo))
@@ -235,7 +262,7 @@
         half, tile_half, kept_tile, q = orthonormal(image, before, lo, scalars, tile_rows)
         before.append(q)
         kept_tiles.append(kept_tile)
-        fetched.append(fetch_pieces(tile_half, wanted_all))
+        fetched.append(fetch_pieces(tile_half, places))
         mapped.append(
             jnp.dot(blocks, half, preferred_element_type=jnp.float32).astype(jnp.bfloat16)
         )

time: 232 us -> 264 us (1.14)
  waiting for transfers between devices: 104 us -> 123 us
  between operations: 4.66 us -> 18.2 us
  blocking collectives: 43.5 us -> 33.5 us
  starting transfers between devices: 27.6 us -> 33.3 us
  matrix products: 8.65 us -> 13.2 us
    all_gather x0 -> x1, waiting for transfers between devices: none -> 40.9 us  [body(): own_all = lax.all_gather(wavefunction[0], 'op', axis=0, tiled=True)]
    all_to_all x1, waiting for transfers between devices: 25.4 us -> 0.01 us  [body(): lax.all_to_all(part.reshape(ops, tile_rows, hi - lo), 'op', 0, 0, tiled=T...]
    ppermute x0 -> x8, waiting for transfers between devices: none -> 11.6 us  [the longest x6 10.4 us: gather_sectors(): lax.ppermute(pair, 'sec', [(i, (i + 2 * step) % size) for i in range(size)])]
    all_to_all x1 -> x0, blocking collectives: 10.3 us -> none  [from_everyone(): lax.all_to_all(jnp.broadcast_to(value[None], (size, *value.shape)), axis,...]
    all_to_all x2 -> x1, waiting for transfers between devices: 55.5 us -> 46.9 us  [from_everyone(): lax.all_to_all(jnp.broadcast_to(value[None], (size, *value.shape)), axis,...]
    ppermute x0 -> x8, starting transfers between devices: none -> 7.63 us  [the longest x6 7.53 us: gather_sectors(): lax.ppermute(pair, 'sec', [(i, (i + 2 * step) % size) for i in range(size)])]
    dot_general x2 -> x4, matrix products: 3.34 us -> 7.85 us  [the longest x2 3.72 us: from_left(): lax.dot_general(jnp.concatenate([left, left], axis=0), jnp.concatenate([h...]
    all_to_all x2 -> x1, starting transfers between devices: 10.3 us -> 7.91 us  [from_everyone(): lax.all_to_all(jnp.broadcast_to(value[None], (size, *value.shape)), axis,...]
  transfers between devices with their start and end apart: 4 -> 12, of which waited for: 4 -> 6; matrix products, arithmetic and copies ran while one was open for 1% -> 5% of each run, Pallas kernels for 0% -> 0%
where the time goes in v3:
time: 264 us
  waiting for transfers between devices  123 us (47%)
  blocking collectives  33.5 us (13%)
  starting transfers between devices  33.3 us (13%)
  Pallas kernels  31.8 us (12%)
  between operations  18.2 us (7%)
  matrix products  13.2 us (5%)
  local copies, waits for them, and re-layouts  7.77 us (3%)
  other arithmetic  3.14 us (1%)
    all_to_all x1, waiting for transfers between devices, from_everyone(): lax.all_to_all(jnp.broadcast_to(value[None], (size, *value.shape)), axis,...  46.9 us
    all_gather x1, waiting for transfers between devices, body(): own_all = lax.all_gather(wavefunction[0], 'op', axis=0, tiled=True)  40.9 us
    all_to_all x1, blocking collectives, fetch_pieces(): incoming = lax.all_to_all(outgoing, 'op', 0, 0, tiled=True)  33.5 us
    pallas_call x1, Pallas kernels, orthonormal(): pl.pallas_call(lambda *refs: basis_kernel(offset, *refs), out_shape=(jax....  31.8 us
    all_to_all x1, waiting for transfers between devices, fetch_pieces(): incoming = lax.all_to_all(outgoing, 'op', 0, 0, tiled=True)  22.8 us
    all_to_all x1, starting transfers between devices, fetch_pieces(): incoming = lax.all_to_all(outgoing, 'op', 0, 0, tiled=True)  11.6 us
    ppermute x6, waiting for transfers between devices, gather_sectors(): lax.ppermute(pair, 'sec', [(i, (i + 2 * step) % size) for i in range(size)])  10.4 us
    all_to_all x1, starting transfers between devices, from_everyone(): lax.all_to_all(jnp.broadcast_to(value[None], (size, *value.shape)), axis,...  7.91 us
  transfers between devices with their start and end apart: 12, of which 6 were waited for; matrix products, arithmetic and copies ran while one was open for 5% of the time, Pallas kernels for 0%

profile of v3, /device:TPU:2, one launch (start us, length us, event | category | flops | bytes accessed | tf_op | source)
XLA Modules:
  0.0 263.5 jit_solution(6899658905092382745)
XLA Ops:
  9.7 3.0 %collective-permute-start.3 = (bf16[2,16,1024]{2,1,0:T(8,128)(2,1)S(1)}, bf16[2,16,1024]{2,1,0:T(8,128)(2,1)S(1)}, u32[]{:S(2)}, u32[]{:S(2)}) collective-permute-start(bf16[2,16,1024]{2,1,0:T(8,128)(2,1)S(1)} %pad_maximum_fusion), channel_id=1, source_target_pairs={{0,192},{32,224},{64,0},{96,32},{128,64},{160,96},{192,128},{224,1... | collective-permute-start | bytes 196616 | tf_op jit(solution)/shard_map/ppermute | solution.py:174
  13.4 1.0 collective-permute-start.1
  14.3 5.4 %collective-permute-done.1 = bf16[2,16,1024]{2,1,0:T(8,128)(2,1)S(1)} collective-permute-done((bf16[2,16,1024]{2,1,0:T(8,128)(2,1)S(1)}, bf16[2,16,1024]{2,1,0:T(8,128)(2,1)S(1)}, u32[]{:S(2)}, u32[]{:S(2)}) %collective-permute-start.1) | collective-permute-done | bytes 65568 | tf_op jit(solution)/shard_map/ppermute | solution.py:174
  19.8 1.6 gather_fusion
  21.4 11.6 %all-to-all-start = ((bf16[32,16,1024]{2,1,0:T(8,128)(2,1)}), bf16[32,16,1024]{2,1,0:T(8,128)(2,1)S(1)}, u32[]{:S(2)}, u32[]{:S(2)}) async-start(bf16[32,16,1024]{2,1,0:T(8,128)(2,1)} %gather_fusion), calls=%async_computation | async-start | bytes 2097152 | tf_op jit(solution)/shard_map/all_to_all | solution.py:187
  38.2 22.8 %all-to-all-done = bf16[32,16,1024]{2,1,0:T(8,128)(2,1)S(1)} async-done(((bf16[32,16,1024]{2,1,0:T(8,128)(2,1)}), bf16[32,16,1024]{2,1,0:T(8,128)(2,1)S(1)}, u32[]{:S(2)}, u32[]{:S(2)}) %all-to-all-start) | async-done | bytes 1048608 | tf_op jit(solution)/shard_map/all_to_all | solution.py:187
  61.1 1.3 fusion.8
  63.2 2.2 fusion.14
  65.4 6.1 %all-to-all-start.1 = ((bf16[32,32,512]{2,1,0:T(8,128)(2,1)}), bf16[32,32,512]{2,1,0:T(8,128)(2,1)S(1)}, u32[]{:S(2)}, u32[]{:S(2)}) async-start(bf16[32,32,512]{2,1,0:T(8,128)(2,1)} %bitcast.55), calls=%async_computation.1 | async-start | bytes 2097152 | tf_op jit(solution)/shard_map/all_to_all | solution.py:255
  72.8 40.9 %all-gather.3.cloned.1.call-done = bf16[1,512,1024]{2,1,0:T(8,128)(2,1)} async-done(((bf16[1,16,1024]{2,1,0:T(8,128)(2,1)}), bf16[1,512,1024]{2,1,0:T(8,128)(2,1)}) %all-gather.3.cloned.1.call-update) | async-done | bytes 1048592 | tf_op jit(solution)/shard_map/all_gather | solution.py:232
  113.7 1.3 bitcast_select_fusion
  115.2 3.3 %subtract_convert_fusion = (bf16[512,512]{1,0:T(8,128)(2,1)}, bf16[512,512]{1,0:T(8,128)(2,1)}) fusion(bf16[1,1024,512]{2,1,0:T(8,128)(2,1)} %param.10, pred[1024]{0:T(1024)(128)(4,1)S(1)} %iota_compare_fusion.1, bf16[1,512,1024]{2,1,0:T(8,128)(2,1)} %all-gather.3.cloned.1.call-done), kind=kOutput, calls=%fused_computation.26 | convolution fusion | flops 538968064 | bytes 3146752 | tf_op jit(solution)/shard_map/dot_general | solution.py:243
  118.7 1.5 fusion.17
  120.2 1.6 broadcast_in_dim.108
  121.8 7.9 %all-to-all-start.2 = ((f32[32,32,512]{2,1,0:T(8,128)}), f32[32,32,512]{2,1,0:T(8,128)}, u32[]{:S(2)}, u32[]{:S(2)}) async-start(f32[32,32,512]{2,1,0:T(8,128)} %broadcast_in_dim.108), calls=%async_computation.2 | async-start | bytes 4194304 | tf_op jit(solution)/shard_map/all_to_all | solution.py:158
  129.8 46.9 %all-to-all-done.2 = f32[32,32,512]{2,1,0:T(8,128)} async-done(((f32[32,32,512]{2,1,0:T(8,128)}), f32[32,32,512]{2,1,0:T(8,128)}, u32[]{:S(2)}, u32[]{:S(2)}) %all-to-all-start.2) | async-done | bytes 2097184 | tf_op jit(solution)/shard_map/all_to_all | solution.py:158
  176.6 31.8 %basis_0.1 = (bf16[1024,512]{1,0:T(8,128)(2,1)S(1)}, bf16[32,512]{1,0:T(8,128)(2,1)S(1)}, f32[32,512]{1,0:T(8,128)}, f32[1024,512]{1,0:T(8,128)}) custom-call(s32[2]{0:T(128)S(1)} %pad_add_fusion.refs_0_, f32[1024,512]{1,0:T(8,128)} %bitcast.18.refs_1_), custom_call_target="tpu_custom_call" | custom-call | flops 40000000000 | bytes 6291456 | tf_op jit(solution)/shard_map/basis_0/pallas_call | solution.py:134
  208.4 1.2 collective-permute-done.4
  209.6 1.2 collective-permute-start.7
  210.8 1.1 collective-permute-start.6
  212.5 5.0 %collective-permute-done.5 = bf16[2,32,512]{2,1,0:T(8,128)(2,1)S(1)} collective-permute-done((bf16[2,32,512]{2,1,0:T(8,128)(2,1)S(1)}, bf16[2,32,512]{2,1,0:T(8,128)(2,1)S(1)}, u32[]{:S(2)}, u32[]{:S(2)}) %collective-permute-start.5) | collective-permute-done | bytes 65568 | tf_op jit(solution)/shard_map/ppermute | solution.py:174
  217.6 1.6 gather_fusion.1
  219.2 33.5 %all_to_all.20 = bf16[32,32,512]{2,1,0:T(8,128)(2,1)} all-to-all(bf16[32,32,512]{2,1,0:T(8,128)(2,1)} %gather_fusion.1), channel_id=1, replica_groups=mesh['sec'=8,'op'=32] {'op'}, dimensions={0} | all-to-all | bytes 2097152 | tf_op jit(solution)/shard_map/all_to_all | solution.py:187
  252.7 4.0 %convolution_bitcast_fusion = f32[1,1,512,512]{3,2,1,0:T(8,128)} fusion(bf16[1024,512]{1,0:T(8,128)(2,1)} %bitcast.56, bf16[1024,512]{1,0:T(8,128)(2,1)S(1)} %get-tuple-element.7, bf16[1,1,1024,1024]{3,2,1,0:T(8,128)(2,1)S(1)} %copy-done), kind=kOutput, calls=%fused_computation.14 | convolution fusion | flops 1611137024 | bytes 5242880 | tf_op jit(solution)/shard_map/dot_general | solution.py:272
  (48 shorter events, 7.8 us)
Async XLA Ops:
  7.2 53.9 %copy-start = (bf16[1,1,1024,1024]{3,2,1,0:T(8,128)(2,1)S(1)}, bf16[1,1,1024,1024]{3,2,1,0:T(8,128)(2,1)}, u32[]{:S(2)}) copy-start(bf16[1,1,1024,1024]{3,2,1,0:T(8,128)(2,1)} %param.9) | copy-start | bytes 6291460
  7.2 1.8 collective-permute-start
  9.7 10.0 %collective-permute-start.3 = (bf16[2,16,1024]{2,1,0:T(8,128)(2,1)S(1)}, bf16[2,16,1024]{2,1,0:T(8,128)(2,1)S(1)}, u32[]{:S(2)}, u32[]{:S(2)}) collective-permute-start(bf16[2,16,1024]{2,1,0:T(8,128)(2,1)S(1)} %pad_maximum_fusion), channel_id=1, source_target_pairs={{0,192},{32,224},{64,0},{96,32},{128,64},{160,96},{192,128},{224,1... | collective-permute-start | bytes 196616 | tf_op jit(solution)/shard_map/ppermute | solution.py:174
  12.7 7.0 %collective-permute-start.2 = (bf16[2,16,1024]{2,1,0:T(8,128)(2,1)S(1)}, bf16[2,16,1024]{2,1,0:T(8,128)(2,1)S(1)}, u32[]{:S(2)}, u32[]{:S(2)}) collective-permute-start(bf16[2,16,1024]{2,1,0:T(8,128)(2,1)S(1)} %pad_maximum_fusion), channel_id=1, source_target_pairs={{0,128},{32,160},{64,192},{96,224},{128,0},{160,32},{192,64},{224,... | collective-permute-start | bytes 196616 | tf_op jit(solution)/shard_map/ppermute | solution.py:174
  13.4 6.3 %collective-permute-start.1 = (bf16[2,16,1024]{2,1,0:T(8,128)(2,1)S(1)}, bf16[2,16,1024]{2,1,0:T(8,128)(2,1)S(1)}, u32[]{:S(2)}, u32[]{:S(2)}) collective-permute-start(bf16[2,16,1024]{2,1,0:T(8,128)(2,1)S(1)} %pad_maximum_fusion), channel_id=1, source_target_pairs={{0,64},{32,96},{64,128},{96,160},{128,192},{160,224},{192,0},{224,... | collective-permute-start | bytes 196616 | tf_op jit(solution)/shard_map/ppermute | solution.py:174
  19.8 16.4 %copy-start.1 = (s32[8]{0:T(128)S(1)}, s32[8]{0:T(128)}, u32[]{:S(2)}) copy-start(s32[8]{0:T(128)} %param.11) | copy-start | bytes 100
  21.4 39.6 %all-to-all-start = ((bf16[32,16,1024]{2,1,0:T(8,128)(2,1)}), bf16[32,16,1024]{2,1,0:T(8,128)(2,1)S(1)}, u32[]{:S(2)}, u32[]{:S(2)}) async-start(bf16[32,16,1024]{2,1,0:T(8,128)(2,1)} %gather_fusion), calls=%async_computation | async-start | bytes 2097152 | tf_op jit(solution)/shard_map/all_to_all | solution.py:187
  33.0 80.7 %all-gather.3.cloned.1.call-start = ((), (), s32[]{:S(2)}) async-start(), calls=%async_computation.4 | async-start | bytes 1081344 | tf_op jit(solution)/shard_map/all_gather | solution.py:232
  61.1 1.3 copy-start.2
  65.4 6.1 %copy-start.3 = (s32[8]{0:T(128)S(1)}, s32[8]{0:T(128)}, u32[]{:S(2)}) copy-start(s32[8]{0:T(128)} %param.12) | copy-start | bytes 100
  65.4 53.1 %all-to-all-start.1 = ((bf16[32,32,512]{2,1,0:T(8,128)(2,1)}), bf16[32,32,512]{2,1,0:T(8,128)(2,1)S(1)}, u32[]{:S(2)}, u32[]{:S(2)}) async-start(bf16[32,32,512]{2,1,0:T(8,128)(2,1)} %bitcast.55), calls=%async_computation.1 | async-start | bytes 2097152 | tf_op jit(solution)/shard_map/all_to_all | solution.py:255
  121.8 54.9 %all-to-all-start.2 = ((f32[32,32,512]{2,1,0:T(8,128)}), f32[32,32,512]{2,1,0:T(8,128)}, u32[]{:S(2)}, u32[]{:S(2)}) async-start(f32[32,32,512]{2,1,0:T(8,128)} %broadcast_in_dim.108), calls=%async_computation.2 | async-start | bytes 4194304 | tf_op jit(solution)/shard_map/all_to_all | solution.py:158
  208.4 1.2 collective-permute-start.4
  209.6 8.0 %collective-permute-start.7 = (bf16[2,32,512]{2,1,0:T(8,128)(2,1)S(1)}, bf16[2,32,512]{2,1,0:T(8,128)(2,1)S(1)}, u32[]{:S(2)}, u32[]{:S(2)}) collective-permute-start(bf16[2,32,512]{2,1,0:T(8,128)(2,1)S(1)} %pad_maximum_fusion.1), channel_id=1, source_target_pairs={{0,192},{32,224},{64,0},{96,32},{128,64},{160,96},{192,128},{224,1... | collective-permute-start | bytes 196616 | tf_op jit(solution)/shard_map/ppermute | solution.py:174
  210.8 6.8 %collective-permute-start.6 = (bf16[2,32,512]{2,1,0:T(8,128)(2,1)S(1)}, bf16[2,32,512]{2,1,0:T(8,128)(2,1)S(1)}, u32[]{:S(2)}, u32[]{:S(2)}) collective-permute-start(bf16[2,32,512]{2,1,0:T(8,128)(2,1)S(1)} %pad_maximum_fusion.1), channel_id=1, source_target_pairs={{0,128},{32,160},{64,192},{96,224},{128,0},{160,32},{192,64},{224,... | collective-permute-start | bytes 196616 | tf_op jit(solution)/shard_map/ppermute | solution.py:174
  211.8 5.7 %collective-permute-start.5 = (bf16[2,32,512]{2,1,0:T(8,128)(2,1)S(1)}, bf16[2,32,512]{2,1,0:T(8,128)(2,1)S(1)}, u32[]{:S(2)}, u32[]{:S(2)}) collective-permute-start(bf16[2,32,512]{2,1,0:T(8,128)(2,1)S(1)} %pad_maximum_fusion.1), channel_id=1, source_target_pairs={{0,64},{32,96},{64,128},{96,160},{128,192},{160,224},{192,0},{224,... | collective-permute-start | bytes 196616 | tf_op jit(solution)/shard_map/ppermute | solution.py:174
Sparse Core Ops, SparseCore 0:
  36.4 77.2 all-gather.2

commit v4 on v3

--- a/solution.py
+++ b/solution.py
@@ -13,6 +13,18 @@
 def dot(a, b, ca, cb):
     return lax.dot_general(
         a, b, (((ca,), (cb,)), ((), ())), precision=HIGHEST, preferred_element_type=jnp.float32
+    )
+
+
+def dot3(a, b, ca, cb):
+    dims = (((ca,), (cb,)), ((), ()))
+    a_high, b_high = a.astype(jnp.bfloat16), b.astype(jnp.bfloat16)
+    a_low = (a - a_high.astype(jnp.float32)).astype(jnp.bfloat16)
+    b_low = (b - b_high.astype(jnp.float32)).astype(jnp.bfloat16)
+    return (
+        lax.dot_general(a_low, b_high, dims, preferred_element_type=jnp.float32)
+        + lax.dot_general(a_high, b_low, dims, preferred_element_type=jnp.float32)
+        + lax.dot_general(a_high, b_high, dims, preferred_element_type=jnp.float32)
     )
 
 
@@ -31,25 +43,21 @@
             v, w = rows[g], aug[g]
             cols = [jnp.broadcast_to(v[:, 8 * g + j:8 * g + j + 1], (8, LANE)) for j in range(8)]
             e = {(i, j): jnp.broadcast_to(cols[j][i:i + 1, :], (8, LANE)) for j in range(8) for i in range(j, 8)}
-            inv, low = [], {}
+            low, m = {}, {}
             for j in range(8):
-                d = e[j, j]
-                r = lax.rsqrt(d)
-                r = r * (1.5 - 0.5 * d * r * r)
-                inv.append(r)
+                r = lax.rsqrt(e[j, j])
+                m[j, j] = r
+                for c in range(j):
+                    m[j, c] = m[j, c] * r
                 for i in range(j + 1, 8):
                     low[i, j] = e[i, j] * r
                 for k in range(j + 1, 8):
                     for i in range(k, 8):
                         e[i, k] = e[i, k] - low[i, j] * low[k, j]
-            m = {}
-            for c in range(8):
-                m[c, c] = inv[c]
-                for i in range(c + 1, 8):
-                    t = low[i, c] * m[c, c]
-                    for k in range(c + 1, i):
-                        t = t + low[i, k] * m[k, c]
-                    m[i, c] = -t * inv[i]
+                for i in range(j + 1, 8):
+                    for c in range(j + 1):
+                        t = low[i, j] * m[j, c]
+                        m[i, c] = m[i, c] - t if (i, c) in m else -t
             rv = rw = None
             mcols = []
             for j in range(8):
@@ -103,16 +111,17 @@
         t_ref[...] = image_ref[...]
     r_i = lax.broadcasted_iota(jnp.int32, (width, width), 0)
     c_i = lax.broadcasted_iota(jnp.int32, (width, width), 1)
-    a_ref[...] = dot(t_ref[...], t_ref[...], 0, 0) + jnp.where(
-        (r_i == c_i) & (c_i + offset >= kept), 1.0, 0.0
-    )
+    ones = jnp.where((r_i == c_i) & (c_i + offset >= kept), 1.0, 0.0)
+    for lo in range(0, width, LANE):
+        hi = lo + LANE
+        a_ref[lo:hi, lo:] = dot3(t_ref[:, lo:hi], t_ref[:, lo:], 0, 0) + ones[lo:hi, lo:]
     for lo in range(0, width, LANE):
         hi = lo + LANE
         inv = factor_block(a_ref[lo:hi, lo:hi])
         t = t_ref[:, lo:hi]
         if lo:
-            t = t - dot(q_ref[:, :lo], a_ref[:lo, lo:hi], 1, 0)
-        q = dot(t, inv, 1, 1)
+            t = t - dot3(q_ref[:, :lo], a_ref[:lo, lo:hi], 1, 0)
+        q = dot3(t, inv, 1, 1)
         q_ref[:, lo:hi] = q
         half_ref[:, lo:hi] = q.astype(jnp.bfloat16)
         if hi < width:
@@ -229,20 +238,18 @@
     own_mask = states < own_size
     source_mask = states < jnp.take(sector_sizes, wanted)
     zero_half = jnp.zeros((), jnp.bfloat16)
-    own_all = lax.all_gather(wavefunction[0], "op", axis=0, tiled=True)
+    own_rows = jnp.where(own_mask[None, :], wavefunction[0], zero_half)
     moved = fetch_pieces(wavefunction[0], places)
     moved = jnp.where(source_mask[None, :], moved, zero_half)
     blocks = op_blocks[0, 0]
     perturbed = jnp.dot(moved, blocks, preferred_element_type=jnp.float32).astype(jnp.bfloat16)
     guess_rows = jnp.where(own_mask[:, None], basis_guess[0], zero_half)
-    proj = noise_weight * jnp.dot(perturbed, guess_rows, preferred_element_type=jnp.float32)
-    proj_high, proj_low = in_halves(proj)
-    own_all = jnp.where(own_mask[None, :], own_all, zero_half)
-    own_columns = lax.dynamic_slice_in_dim(own_all, op_index * tile_rows, tile_rows, 1)
-    own_high, own_low = in_halves(
-        jnp.dot(own_all, guess_rows, preferred_element_type=jnp.float32)
-    )
-    own_image = from_left(own_columns, own_high, own_low)
+    left = jnp.concatenate([perturbed, own_rows], axis=0)
+    proj = jnp.dot(left, guess_rows, preferred_element_type=jnp.float32)
+    is_noise = jnp.arange(left.shape[0]) < perturbed.shape[0]
+    proj_high, proj_low = in_halves(
+        proj * jnp.where(is_noise, noise_weight, jnp.float32(1.0))[:, None]
+    )
     scalars = jnp.stack([own_kept, op_index])
     row_ids = op_index * tile_rows + jnp.arange(tile_rows, dtype=jnp.int32)
     row_mask = row_ids < own_size
@@ -251,9 +258,9 @@
     images = []
     sums = []
     for lo, hi in cuts:
-        part = from_left(perturbed, proj_high[:, lo:hi], proj_low[:, lo:hi]).astype(jnp.bfloat16)
+        part = from_left(left, proj_high[:, lo:hi], proj_low[:, lo:hi]).astype(jnp.bfloat16)
         tiles = lax.all_to_all(part.reshape(ops, tile_rows, hi - lo), "op", 0, 0, tiled=True)
-        sums.append(jnp.sum(tiles.astype(jnp.float32), axis=0) + own_image[:, lo:hi])
+        sums.append(jnp.sum(tiles.astype(jnp.float32), axis=0))
     for (lo, hi), total in zip(cuts, sums):
         image = jnp.where(row_mask[:, None] & col_mask[None, lo:hi], total, jnp.float32(0.0))
         images.append(from_everyone(image, "op").reshape(state_count, hi - lo))
@@ -264,7 +271,9 @@
         kept_tiles.append(kept_tile)
         fetched.append(fetch_pieces(tile_half, places))
         mapped.append(
-            jnp.dot(blocks, half, preferred_element_type=jnp.float32).astype(jnp.bfloat16)
+            lax.optimization_barrier(
+                jnp.dot(blocks, half, preferred_element_type=jnp.float32).astype(jnp.bfloat16)
+            )
         )
     mapped = jnp.concatenate(mapped, axis=1)
     rotated = jnp.concatenate(

time: 264 us -> 222 us (0.84)
  blocking collectives: 33.5 us -> 0 us
  between operations: 18.2 us -> 4.8 us
  waiting for transfers between devices: 123 us -> 135 us
  Pallas kernels: 31.8 us -> 26.4 us
  matrix products: 13.2 us -> 10.2 us
    all_gather x1 -> x0, waiting for transfers between devices: 40.9 us -> none  [body(): own_all = lax.all_gather(wavefunction[0], 'op', axis=0, tiled=True)]
    all_to_all x1 -> x0, blocking collectives: 33.5 us -> none  [fetch_pieces(): incoming = lax.all_to_all(outgoing, 'op', 0, 0, tiled=True)]
    all_to_all x1 -> x2, waiting for transfers between devices: 22.8 us -> 49.1 us  [fetch_pieces(): incoming = lax.all_to_all(outgoing, 'op', 0, 0, tiled=True)]
    all_to_all x1, waiting for transfers between devices: 0.01 us -> 25.4 us  [body(): lax.all_to_all(part.reshape(ops, tile_rows, hi - lo), 'op', 0, 0, tiled=T...]
    all_to_all x1 -> x2, starting transfers between devices: 11.6 us -> 17.2 us  [fetch_pieces(): incoming = lax.all_to_all(outgoing, 'op', 0, 0, tiled=True)]
    pallas_call x1, Pallas kernels: 31.8 us -> 26.4 us  [orthonormal(): pl.pallas_call(lambda *refs: basis_kernel(offset, *refs), out_shape=(jax....]
  transfers between devices with their start and end apart: 12 -> 12, of which waited for: 6 -> 7; matrix products, arithmetic and copies ran while one was open for 5% -> 3% of each run, Pallas kernels for 0% -> 0%
where the time goes in v4:
time: 222 us
  waiting for transfers between devices  135 us (61%)
  starting transfers between devices  35.6 us (16%)
  Pallas kernels  26.4 us (12%)
  matrix products  10.2 us (5%)
  local copies, waits for them, and re-layouts  7.59 us (3%)
  between operations  4.8 us (2%)
    all_to_all x2, waiting for transfers between devices, fetch_pieces(): incoming = lax.all_to_all(outgoing, 'op', 0, 0, tiled=True)  49.1 us
    all_to_all x1, waiting for transfers between devices, from_everyone(): lax.all_to_all(jnp.broadcast_to(value[None], (size, *value.shape)), axis,...  48.7 us
    pallas_call x1, Pallas kernels, orthonormal(): pl.pallas_call(lambda *refs: basis_kernel(offset, *refs), out_shape=(jax....  26.4 us
    all_to_all x1, waiting for transfers between devices, body(): lax.all_to_all(part.reshape(ops, tile_rows, hi - lo), 'op', 0, 0, tiled=T...  25.4 us
    all_to_all x2, starting transfers between devices, fetch_pieces(): incoming = lax.all_to_all(outgoing, 'op', 0, 0, tiled=True)  17.2 us
    ppermute x6, waiting for transfers between devices, gather_sectors(): lax.ppermute(pair, 'sec', [(i, (i + 2 * step) % size) for i in range(size)])  10.6 us
    ppermute x6, starting transfers between devices, gather_sectors(): lax.ppermute(pair, 'sec', [(i, (i + 2 * step) % size) for i in range(size)])  6.73 us
    all_to_all x1, starting transfers between devices, from_everyone(): lax.all_to_all(jnp.broadcast_to(value[None], (size, *value.shape)), axis,...  5.8 us
  transfers between devices with their start and end apart: 12, of which 7 were waited for; matrix products, arithmetic and copies ran while one was open for 3% of the time, Pallas kernels for 0%

profile of v4, /device:TPU:2, one launch (start us, length us, event | category | flops | bytes accessed | tf_op | source)
XLA Modules:
  0.0 221.5 jit_solution(18241971019717836158)
XLA Ops:
  0.8 0.9 constant_dynamic-update-slice_fusion.4
  3.2 3.0 %collective-permute-start.3 = (bf16[2,16,1024]{2,1,0:T(8,128)(2,1)S(1)}, bf16[2,16,1024]{2,1,0:T(8,128)(2,1)S(1)}, u32[]{:S(2)}, u32[]{:S(2)}) collective-permute-start(bf16[2,16,1024]{2,1,0:T(8,128)(2,1)S(1)} %pad_maximum_fusion), channel_id=1, source_target_pairs={{0,192},{32,224},{64,0},{96,32},{128,64},{160,96},{192,128},{224,1... | collective-permute-start | bytes 196616 | tf_op jit(solution)/shard_map/ppermute | solution.py:183
  6.8 1.0 collective-permute-start.1
  7.8 5.4 %collective-permute-done.1 = bf16[2,16,1024]{2,1,0:T(8,128)(2,1)S(1)} collective-permute-done((bf16[2,16,1024]{2,1,0:T(8,128)(2,1)S(1)}, bf16[2,16,1024]{2,1,0:T(8,128)(2,1)S(1)}, u32[]{:S(2)}, u32[]{:S(2)}) %collective-permute-start.1) | collective-permute-done | bytes 65568 | tf_op jit(solution)/shard_map/ppermute | solution.py:183
  13.3 1.6 gather_fusion
  14.8 11.6 %all-to-all-start = ((bf16[32,16,1024]{2,1,0:T(8,128)(2,1)}), bf16[32,16,1024]{2,1,0:T(8,128)(2,1)S(1)}, u32[]{:S(2)}, u32[]{:S(2)}) async-start(bf16[32,16,1024]{2,1,0:T(8,128)(2,1)} %gather_fusion), calls=%async_computation | async-start | bytes 2097152 | tf_op jit(solution)/shard_map/all_to_all | solution.py:196
  30.9 23.5 %all-to-all-done = bf16[32,16,1024]{2,1,0:T(8,128)(2,1)S(1)} async-done(((bf16[32,16,1024]{2,1,0:T(8,128)(2,1)}), bf16[32,16,1024]{2,1,0:T(8,128)(2,1)S(1)}, u32[]{:S(2)}, u32[]{:S(2)}) %all-to-all-start) | async-done | bytes 1048608 | tf_op jit(solution)/shard_map/all_to_all | solution.py:196
  54.5 1.3 fusion.12
  55.8 0.8 subtract_convert_fusion
  56.6 2.5 %fusion.18 = bf16[1024,512]{1,0:T(8,128)(2,1)} fusion(bf16[16,1024]{1,0:T(8,128)(2,1)S(1)} %broadcast_select_fusion.1, bf16[512,1024]{1,0:T(8,128)(2,1)S(1)} %fusion.12, bf16[528,512]{1,0:T(8,128)(2,1)S(1)} %get-tuple-element.63, bf16[528,512]{1,0:T(8,128)(2,1)S(1)} %get-tuple-element.64), kind=kOutput, calls=%fused_computation.17 | convolution fusion | flops 1118633984 | bytes 3211264 | tf_op jit(solution)/shard_map/dot_general | solution.py:206
  59.1 5.7 %all-to-all-start.1 = ((bf16[32,32,512]{2,1,0:T(8,128)(2,1)}), bf16[32,32,512]{2,1,0:T(8,128)(2,1)S(1)}, u32[]{:S(2)}, u32[]{:S(2)}) async-start(bf16[32,32,512]{2,1,0:T(8,128)(2,1)} %bitcast.50), calls=%async_computation.1 | async-start | bytes 2097152 | tf_op jit(solution)/shard_map/all_to_all | solution.py:262
  66.3 25.4 %all-to-all-done.1 = bf16[32,32,512]{2,1,0:T(8,128)(2,1)S(1)} async-done(((bf16[32,32,512]{2,1,0:T(8,128)(2,1)}), bf16[32,32,512]{2,1,0:T(8,128)(2,1)S(1)}, u32[]{:S(2)}, u32[]{:S(2)}) %all-to-all-start.1) | async-done | bytes 1048608 | tf_op jit(solution)/shard_map/all_to_all | solution.py:262
  91.9 1.6 broadcast_in_dim.123
  93.5 5.8 %all-to-all-start.2 = ((f32[32,32,512]{2,1,0:T(8,128)}), f32[32,32,512]{2,1,0:T(8,128)}, u32[]{:S(2)}, u32[]{:S(2)}) async-start(f32[32,32,512]{2,1,0:T(8,128)} %broadcast_in_dim.123), calls=%async_computation.2 | async-start | bytes 4194304 | tf_op jit(solution)/shard_map/all_to_all | solution.py:167
  99.4 48.7 %all-to-all-done.2 = f32[32,32,512]{2,1,0:T(8,128)} async-done(((f32[32,32,512]{2,1,0:T(8,128)}), f32[32,32,512]{2,1,0:T(8,128)}, u32[]{:S(2)}, u32[]{:S(2)}) %all-to-all-start.2) | async-done | bytes 2097184 | tf_op jit(solution)/shard_map/all_to_all | solution.py:167
  148.1 26.4 %basis_0.1 = (bf16[1024,512]{1,0:T(8,128)(2,1)S(1)}, bf16[32,512]{1,0:T(8,128)(2,1)S(1)}, f32[32,512]{1,0:T(8,128)}, f32[1024,512]{1,0:T(8,128)}) custom-call(s32[2]{0:T(128)S(1)} %pad_add_fusion.refs_0_, f32[1024,512]{1,0:T(8,128)} %bitcast.17.refs_1_), custom_call_target="tpu_custom_call" | custom-call | flops 40000000000 | bytes 6291456 | tf_op jit(solution)/shard_map/basis_0/pallas_call | solution.py:143
  174.5 1.2 collective-permute-done.4
  176.5 1.3 collective-permute-start.5
  177.8 5.2 %collective-permute-done.5 = bf16[2,32,512]{2,1,0:T(8,128)(2,1)S(1)} collective-permute-done((bf16[2,32,512]{2,1,0:T(8,128)(2,1)S(1)}, bf16[2,32,512]{2,1,0:T(8,128)(2,1)S(1)}, u32[]{:S(2)}, u32[]{:S(2)}) %collective-permute-start.5) | collective-permute-done | bytes 65568 | tf_op jit(solution)/shard_map/ppermute | solution.py:183
  183.1 1.6 gather_fusion.1
  184.7 5.6 %all-to-all-start.3 = ((bf16[32,32,512]{2,1,0:T(8,128)(2,1)}), bf16[32,32,512]{2,1,0:T(8,128)(2,1)}, u32[]{:S(2)}, u32[]{:S(2)}) async-start(bf16[32,32,512]{2,1,0:T(8,128)(2,1)} %gather_fusion.1), calls=%async_computation.3 | async-start | bytes 2097152 | tf_op jit(solution)/shard_map/all_to_all | solution.py:196
  190.3 2.3 %fusion.21 = bf16[1024,512]{0,1:T(8,128)(2,1)} fusion(bf16[1024,512]{1,0:T(8,128)(2,1)S(1)} %get-tuple-element.7, bf16[1,1,1024,1024]{3,2,1,0:T(8,128)(2,1)S(1)} %copy-done), kind=kOutput, calls=%fused_computation.19 | convolution fusion | flops 1074266112 | bytes 4194304 | tf_op jit(solution)/shard_map/dot_general | solution.py:275
  192.6 25.6 %all-to-all-done.3 = bf16[32,32,512]{2,1,0:T(8,128)(2,1)} async-done(((bf16[32,32,512]{2,1,0:T(8,128)(2,1)}), bf16[32,32,512]{2,1,0:T(8,128)(2,1)}, u32[]{:S(2)}, u32[]{:S(2)}) %all-to-all-start.3) | async-done | bytes 1048608 | tf_op jit(solution)/shard_map/all_to_all | solution.py:196
  218.2 3.3 %convolution_bitcast_fusion = f32[1,1,512,512]{3,2,1,0:T(8,128)} fusion(bf16[1024,512]{1,0:T(8,128)(2,1)} %bitcast.21, bf16[1024,512]{0,1:T(8,128)(2,1)} %fusion.21), kind=kOutput, calls=%fused_computation.20 | convolution fusion | flops 536870912 | bytes 3145728 | tf_op jit(solution)/shard_map/dot_general | solution.py:281
  (47 shorter events, 5.4 us)
Async XLA Ops:
  0.6 53.9 %copy-start = (bf16[1,1,1024,1024]{3,2,1,0:T(8,128)(2,1)S(1)}, bf16[1,1,1024,1024]{3,2,1,0:T(8,128)(2,1)}, u32[]{:S(2)}) copy-start(bf16[1,1,1024,1024]{3,2,1,0:T(8,128)(2,1)} %param.9) | copy-start | bytes 6291460
  0.6 1.8 collective-permute-start
  3.2 10.0 %collective-permute-start.3 = (bf16[2,16,1024]{2,1,0:T(8,128)(2,1)S(1)}, bf16[2,16,1024]{2,1,0:T(8,128)(2,1)S(1)}, u32[]{:S(2)}, u32[]{:S(2)}) collective-permute-start(bf16[2,16,1024]{2,1,0:T(8,128)(2,1)S(1)} %pad_maximum_fusion), channel_id=1, source_target_pairs={{0,192},{32,224},{64,0},{96,32},{128,64},{160,96},{192,128},{224,1... | collective-permute-start | bytes 196616 | tf_op jit(solution)/shard_map/ppermute | solution.py:183
  6.2 7.0 %collective-permute-start.2 = (bf16[2,16,1024]{2,1,0:T(8,128)(2,1)S(1)}, bf16[2,16,1024]{2,1,0:T(8,128)(2,1)S(1)}, u32[]{:S(2)}, u32[]{:S(2)}) collective-permute-start(bf16[2,16,1024]{2,1,0:T(8,128)(2,1)S(1)} %pad_maximum_fusion), channel_id=1, source_target_pairs={{0,128},{32,160},{64,192},{96,224},{128,0},{160,32},{192,64},{224,... | collective-permute-start | bytes 196616 | tf_op jit(solution)/shard_map/ppermute | solution.py:183
  6.8 6.3 %collective-permute-start.1 = (bf16[2,16,1024]{2,1,0:T(8,128)(2,1)S(1)}, bf16[2,16,1024]{2,1,0:T(8,128)(2,1)S(1)}, u32[]{:S(2)}, u32[]{:S(2)}) collective-permute-start(bf16[2,16,1024]{2,1,0:T(8,128)(2,1)S(1)} %pad_maximum_fusion), channel_id=1, source_target_pairs={{0,64},{32,96},{64,128},{96,160},{128,192},{160,224},{192,0},{224,... | collective-permute-start | bytes 196616 | tf_op jit(solution)/shard_map/ppermute | solution.py:183
  13.2 15.7 %copy-start.2 = (s32[8]{0:T(128)S(1)}, s32[8]{0:T(128)}, u32[]{:S(2)}) copy-start(s32[8]{0:T(128)} %param.11) | copy-start | bytes 100
  13.2 17.7 %copy-start.1 = (bf16[1,16,1024]{2,1,0:T(8,128)(2,1)S(1)}, bf16[1,16,1024]{2,1,0:T(8,128)(2,1)}, u32[]{:S(2)}) copy-start(bf16[1,16,1024]{2,1,0:T(8,128)(2,1)} %param.8) | copy-start | bytes 98308
  14.8 39.6 %all-to-all-start = ((bf16[32,16,1024]{2,1,0:T(8,128)(2,1)}), bf16[32,16,1024]{2,1,0:T(8,128)(2,1)S(1)}, u32[]{:S(2)}, u32[]{:S(2)}) async-start(bf16[32,16,1024]{2,1,0:T(8,128)(2,1)} %gather_fusion), calls=%async_computation | async-start | bytes 2097152 | tf_op jit(solution)/shard_map/all_to_all | solution.py:196
  54.5 1.3 copy-start.3
  59.1 5.7 %copy-start.4 = (s32[8]{0:T(128)S(1)}, s32[8]{0:T(128)}, u32[]{:S(2)}) copy-start(s32[8]{0:T(128)} %param.12) | copy-start | bytes 100
  59.1 32.5 %all-to-all-start.1 = ((bf16[32,32,512]{2,1,0:T(8,128)(2,1)}), bf16[32,32,512]{2,1,0:T(8,128)(2,1)S(1)}, u32[]{:S(2)}, u32[]{:S(2)}) async-start(bf16[32,32,512]{2,1,0:T(8,128)(2,1)} %bitcast.50), calls=%async_computation.1 | async-start | bytes 2097152 | tf_op jit(solution)/shard_map/all_to_all | solution.py:262
  93.5 54.6 %all-to-all-start.2 = ((f32[32,32,512]{2,1,0:T(8,128)}), f32[32,32,512]{2,1,0:T(8,128)}, u32[]{:S(2)}, u32[]{:S(2)}) async-start(f32[32,32,512]{2,1,0:T(8,128)} %broadcast_in_dim.123), calls=%async_computation.2 | async-start | bytes 4194304 | tf_op jit(solution)/shard_map/all_to_all | solution.py:167
  174.5 1.2 collective-permute-start.4
  175.7 7.3 %collective-permute-start.7 = (bf16[2,32,512]{2,1,0:T(8,128)(2,1)S(1)}, bf16[2,32,512]{2,1,0:T(8,128)(2,1)S(1)}, u32[]{:S(2)}, u32[]{:S(2)}) collective-permute-start(bf16[2,32,512]{2,1,0:T(8,128)(2,1)S(1)} %pad_maximum_fusion.1), channel_id=1, source_target_pairs={{0,192},{32,224},{64,0},{96,32},{128,64},{160,96},{192,128},{224,1... | collective-permute-start | bytes 196616 | tf_op jit(solution)/shard_map/ppermute | solution.py:183
  175.8 7.2 %collective-permute-start.6 = (bf16[2,32,512]{2,1,0:T(8,128)(2,1)S(1)}, bf16[2,32,512]{2,1,0:T(8,128)(2,1)S(1)}, u32[]{:S(2)}, u32[]{:S(2)}) collective-permute-start(bf16[2,32,512]{2,1,0:T(8,128)(2,1)S(1)} %pad_maximum_fusion.1), channel_id=1, source_target_pairs={{0,128},{32,160},{64,192},{96,224},{128,0},{160,32},{192,64},{224,... | collective-permute-start | bytes 196616 | tf_op jit(solution)/shard_map/ppermute | solution.py:183
  176.5 6.5 %collective-permute-start.5 = (bf16[2,32,512]{2,1,0:T(8,128)(2,1)S(1)}, bf16[2,32,512]{2,1,0:T(8,128)(2,1)S(1)}, u32[]{:S(2)}, u32[]{:S(2)}) collective-permute-start(bf16[2,32,512]{2,1,0:T(8,128)(2,1)S(1)} %pad_maximum_fusion.1), channel_id=1, source_target_pairs={{0,64},{32,96},{64,128},{96,160},{128,192},{160,224},{192,0},{224,... | collective-permute-start | bytes 196616 | tf_op jit(solution)/shard_map/ppermute | solution.py:183
  184.7 33.6 %all-to-all-start.3 = ((bf16[32,32,512]{2,1,0:T(8,128)(2,1)}), bf16[32,32,512]{2,1,0:T(8,128)(2,1)}, u32[]{:S(2)}, u32[]{:S(2)}) async-start(bf16[32,32,512]{2,1,0:T(8,128)(2,1)} %gather_fusion.1), calls=%async_computation.3 | async-start | bytes 2097152 | tf_op jit(solution)/shard_map/all_to_all | solution.py:196

commit v5 on v4

--- a/solution.py
+++ b/solution.py
@@ -7,7 +7,6 @@
 
 HIGHEST = lax.Precision.HIGHEST
 LANE = 128
-CUTS = (0, 512)
 
 
 def dot(a, b, ca, cb):
@@ -95,23 +94,15 @@
     return jnp.concatenate(out, axis=0)
 
 
-def basis_kernel(offset, scalars_ref, image_ref, *refs):
-    count = len(refs) - 6
-    before = refs[:count]
-    half_ref, tile_half_ref, kept_ref, q_ref, a_ref, t_ref = refs[count:]
-    rows, width = image_ref.shape
+def basis_kernel(scalars_ref, *refs):
+    blocks, (half_ref, tile_half_ref, kept_ref, q_ref, a_ref, t_ref) = refs[:-6], refs[-6:]
+    rows, width = t_ref.shape
     kept, own = scalars_ref[0], scalars_ref[1]
-    if before:
-        t_ref[...] = image_ref[...]
-        for earlier in before:
-            t_ref[...] = t_ref[...] - dot(
-                earlier[...], dot(earlier[...], image_ref[...], 0, 0), 1, 0
-            )
-    else:
-        t_ref[...] = image_ref[...]
+    for b, block in enumerate(blocks):
+        t_ref[:, b * LANE : (b + 1) * LANE] = block[...]
     r_i = lax.broadcasted_iota(jnp.int32, (width, width), 0)
     c_i = lax.broadcasted_iota(jnp.int32, (width, width), 1)
-    ones = jnp.where((r_i == c_i) & (c_i + offset >= kept), 1.0, 0.0)
+    ones = jnp.where((r_i == c_i) & (c_i >= kept), 1.0, 0.0)
     for lo in range(0, width, LANE):
         hi = lo + LANE
         a_ref[lo:hi, lo:] = dot3(t_ref[:, lo:hi], t_ref[:, lo:], 0, 0) + ones[lo:hi, lo:]
@@ -137,29 +128,29 @@
     kept_ref[...] = mine * float(rows) ** 0.5
 
 
-def orthonormal(image, before, offset, scalars, tile):
-    rows, width = image.shape
+def orthonormal(blocks, scalars, tile):
+    rows, width = blocks[0].shape[0], len(blocks) * LANE
     vmem = pl.BlockSpec(memory_space=pltpu.VMEM)
     return pl.pallas_call(
-        lambda *refs: basis_kernel(offset, *refs),
+        basis_kernel,
         out_shape=(
             jax.ShapeDtypeStruct((rows, width), jnp.bfloat16),
             jax.ShapeDtypeStruct((tile, width), jnp.bfloat16),
             jax.ShapeDtypeStruct((tile, width), jnp.float32),
-            jax.ShapeDtypeStruct((rows, width), jnp.float32),
         ),
-        in_specs=[pl.BlockSpec(memory_space=pltpu.SMEM)] + [vmem] * (1 + len(before)),
-        out_specs=(vmem,) * 4,
+        in_specs=[pl.BlockSpec(memory_space=pltpu.SMEM)] + [vmem] * len(blocks),
+        out_specs=(vmem,) * 3,
         scratch_shapes=[
+            pltpu.VMEM((rows, width), jnp.float32),
             pltpu.VMEM((width, width), jnp.float32),
             pltpu.VMEM((rows, width), jnp.float32),
         ],
         compiler_params=pltpu.CompilerParams(vmem_limit_bytes=40 << 20),
         cost_estimate=pl.CostEstimate(
-            flops=40_000_000_000 * width // 512, bytes_accessed=rows * width * 12, transcendentals=0
+            flops=5_000_000_000, bytes_accessed=rows * width * 6, transcendentals=0
         ),
-        name="basis_%d" % offset,
-    )(scalars, image, *before)
+        name="orthonormal",
+    )(scalars, *blocks)
 
 
 def from_everyone(value, axis):
@@ -167,6 +158,25 @@
     return lax.all_to_all(
         jnp.broadcast_to(value[None], (size, *value.shape)), axis, 0, 0, tiled=True
     )
+
+
+def gathered_rows(tile):
+    rows, width = tile.shape
+    top = jnp.max(jnp.abs(tile))
+    power = jnp.floor(jnp.log2(jnp.maximum(top, jnp.float32(1e-30))))
+    scaled = (tile * jnp.exp2(12.0 - power)).astype(jnp.float16)
+    sent = jnp.concatenate(
+        [scaled[:, lo : lo + LANE] for lo in range(0, width, LANE)]
+        + [jnp.full((16, LANE), power, jnp.float32).astype(jnp.float16)],
+        axis=0,
+    )
+    got = from_everyone(sent, "op")
+    end = width // LANE * rows
+    scale = jnp.exp2(got[:, end : end + 1, :1].astype(jnp.float32) - 12.0)
+    return [
+        (got[:, lo : lo + rows].astype(jnp.float32) * scale).reshape(-1, LANE)
+        for lo in range(0, end, rows)
+    ]
 
 
 def source_sectors(target_map):
@@ -254,38 +264,22 @@
     row_ids = op_index * tile_rows + jnp.arange(tile_rows, dtype=jnp.int32)
     row_mask = row_ids < own_size
     col_mask = jnp.arange(kept_width, dtype=jnp.int32) < own_kept
-    cuts = list(zip(CUTS[:-1], CUTS[1:]))
-    images = []
-    sums = []
-    for lo, hi in cuts:
-        part = from_left(left, proj_high[:, lo:hi], proj_low[:, lo:hi]).astype(jnp.bfloat16)
-        tiles = lax.all_to_all(part.reshape(ops, tile_rows, hi - lo), "op", 0, 0, tiled=True)
-        sums.append(jnp.sum(tiles.astype(jnp.float32), axis=0))
-    for (lo, hi), total in zip(cuts, sums):
-        image = jnp.where(row_mask[:, None] & col_mask[None, lo:hi], total, jnp.float32(0.0))
-        images.append(from_everyone(image, "op").reshape(state_count, hi - lo))
-    before, kept_tiles, mapped, fetched = [], [], [], []
-    for (lo, hi), image in zip(cuts, images):
-        half, tile_half, kept_tile, q = orthonormal(image, before, lo, scalars, tile_rows)
-        before.append(q)
-        kept_tiles.append(kept_tile)
-        fetched.append(fetch_pieces(tile_half, places))
-        mapped.append(
-            lax.optimization_barrier(
-                jnp.dot(blocks, half, preferred_element_type=jnp.float32).astype(jnp.bfloat16)
-            )
-        )
-    mapped = jnp.concatenate(mapped, axis=1)
-    rotated = jnp.concatenate(
-        [
-            lax.dot_general(
-                source, mapped, (((0,), (0,)), ((), ())), preferred_element_type=jnp.float32
-            )
-            for source in fetched
-        ],
-        axis=0,
-    )
-    return (jnp.concatenate(kept_tiles, axis=1)[None], rotated[None, None])
+    part = from_left(left, proj_high, proj_low).astype(jnp.bfloat16)
+    tiles = lax.all_to_all(part.reshape(ops, tile_rows, kept_width), "op", 0, 0, tiled=True)
+    image = jnp.where(
+        row_mask[:, None] & col_mask[None, :],
+        jnp.sum(tiles.astype(jnp.float32), axis=0),
+        jnp.float32(0.0),
+    )
+    half, tile_half, kept_tile = orthonormal(gathered_rows(image), scalars, tile_rows)
+    mapped = lax.optimization_barrier(
+        jnp.dot(blocks, half, preferred_element_type=jnp.float32).astype(jnp.bfloat16)
+    )
+    source_basis = fetch_pieces(tile_half, places)
+    rotated = lax.dot_general(
+        source_basis, mapped, (((0,), (0,)), ((), ())), preferred_element_type=jnp.float32
+    )
+    return (kept_tile[None], rotated[None, None])
 
 
 def solution(mesh):

time: 222 us -> 202 us (0.910)
  waiting for transfers between devices: 135 us -> 115 us
    all_to_all x1, waiting for transfers between devices: 48.7 us -> 28.6 us  [from_everyone(): lax.all_to_all(jnp.broadcast_to(value[None], (size, *value.shape)), axis,...]
where the time goes in v5:
time: 202 us
  waiting for transfers between devices  115 us (57%)
  starting transfers between devices  35.9 us (18%)
  Pallas kernels  24.7 us (12%)
  matrix products  10.2 us (5%)
  local copies, waits for them, and re-layouts  7.4 us (4%)
  between operations  5.56 us (3%)
  other arithmetic  2.87 us (1%)
    all_to_all x2, waiting for transfers between devices, fetch_pieces(): incoming = lax.all_to_all(outgoing, 'op', 0, 0, tiled=True)  48.9 us
    all_to_all x1, waiting for transfers between devices, from_everyone(): lax.all_to_all(jnp.broadcast_to(value[None], (size, *value.shape)), axis,...  28.6 us
    all_to_all x1, waiting for transfers between devices, body(): lax.all_to_all(part.reshape(ops, tile_rows, kept_width), 'op', 0, 0, tile...  25.7 us
    pallas_call x1, Pallas kernels, orthonormal(): pl.pallas_call(basis_kernel, out_shape=(jax.ShapeDtypeStruct((rows, width...  24.7 us
    all_to_all x2, starting transfers between devices, fetch_pieces(): incoming = lax.all_to_all(outgoing, 'op', 0, 0, tiled=True)  17.6 us
    ppermute x6, waiting for transfers between devices, gather_sectors(): lax.ppermute(pair, 'sec', [(i, (i + 2 * step) % size) for i in range(size)])  10.6 us
    ppermute x6, starting transfers between devices, gather_sectors(): lax.ppermute(pair, 'sec', [(i, (i + 2 * step) % size) for i in range(size)])  6.73 us
    all_to_all x1, starting transfers between devices, from_everyone(): lax.all_to_all(jnp.broadcast_to(value[None], (size, *value.shape)), axis,...  5.74 us
  transfers between devices with their start and end apart: 12, of which 7 were waited for; matrix products, arithmetic and copies ran while one was open for 3% of the time, Pallas kernels for 0%

profile of v5, /device:TPU:2, one launch (start us, length us, event | category | flops | bytes accessed | tf_op | source)
XLA Modules:
  0.0 201.5 jit_solution(9374604638503451735)
XLA Ops:
  0.8 0.9 constant_dynamic-update-slice_fusion.4
  3.2 3.0 %collective-permute-start.3 = (bf16[2,16,1024]{2,1,0:T(8,128)(2,1)S(1)}, bf16[2,16,1024]{2,1,0:T(8,128)(2,1)S(1)}, u32[]{:S(2)}, u32[]{:S(2)}) collective-permute-start(bf16[2,16,1024]{2,1,0:T(8,128)(2,1)S(1)} %pad_maximum_fusion), channel_id=1, source_target_pairs={{0,192},{32,224},{64,0},{96,32},{128,64},{160,96},{192,128},{224,1... | collective-permute-start | bytes 196616 | tf_op jit(solution)/shard_map/ppermute | solution.py:193
  6.8 1.0 collective-permute-start.1
  7.8 5.4 %collective-permute-done.1 = bf16[2,16,1024]{2,1,0:T(8,128)(2,1)S(1)} collective-permute-done((bf16[2,16,1024]{2,1,0:T(8,128)(2,1)S(1)}, bf16[2,16,1024]{2,1,0:T(8,128)(2,1)S(1)}, u32[]{:S(2)}, u32[]{:S(2)}) %collective-permute-start.1) | collective-permute-done | bytes 65568 | tf_op jit(solution)/shard_map/ppermute | solution.py:193
  13.3 1.6 gather_fusion
  14.8 11.6 %all-to-all-start = ((bf16[32,16,1024]{2,1,0:T(8,128)(2,1)}), bf16[32,16,1024]{2,1,0:T(8,128)(2,1)S(1)}, u32[]{:S(2)}, u32[]{:S(2)}) async-start(bf16[32,16,1024]{2,1,0:T(8,128)(2,1)} %gather_fusion), calls=%async_computation | async-start | bytes 2097152 | tf_op jit(solution)/shard_map/all_to_all | solution.py:206
  31.2 23.3 %all-to-all-done = bf16[32,16,1024]{2,1,0:T(8,128)(2,1)S(1)} async-done(((bf16[32,16,1024]{2,1,0:T(8,128)(2,1)}), bf16[32,16,1024]{2,1,0:T(8,128)(2,1)S(1)}, u32[]{:S(2)}, u32[]{:S(2)}) %all-to-all-start) | async-done | bytes 1048608 | tf_op jit(solution)/shard_map/all_to_all | solution.py:206
  54.5 1.3 fusion.12
  55.8 0.8 subtract_convert_fusion
  56.6 2.5 %fusion.18 = bf16[1024,512]{1,0:T(8,128)(2,1)} fusion(bf16[16,1024]{1,0:T(8,128)(2,1)S(1)} %broadcast_select_fusion.1, bf16[512,1024]{1,0:T(8,128)(2,1)S(1)} %fusion.12, bf16[528,512]{1,0:T(8,128)(2,1)S(1)} %get-tuple-element.63, bf16[528,512]{1,0:T(8,128)(2,1)S(1)} %get-tuple-element.64), kind=kOutput, calls=%fused_computation.17 | convolution fusion | flops 1118633984 | bytes 3211264 | tf_op jit(solution)/shard_map/dot_general | solution.py:216
  59.1 5.7 %all-to-all-start.1 = ((bf16[32,32,512]{2,1,0:T(8,128)(2,1)}), bf16[32,32,512]{2,1,0:T(8,128)(2,1)S(1)}, u32[]{:S(2)}, u32[]{:S(2)}) async-start(bf16[32,32,512]{2,1,0:T(8,128)(2,1)} %bitcast.59), calls=%async_computation.1 | async-start | bytes 2097152 | tf_op jit(solution)/shard_map/all_to_all | solution.py:268
  66.0 25.7 %all-to-all-done.1 = bf16[32,32,512]{2,1,0:T(8,128)(2,1)S(1)} async-done(((bf16[32,32,512]{2,1,0:T(8,128)(2,1)}), bf16[32,32,512]{2,1,0:T(8,128)(2,1)S(1)}, u32[]{:S(2)}, u32[]{:S(2)}) %all-to-all-start.1) | async-done | bytes 1048608 | tf_op jit(solution)/shard_map/all_to_all | solution.py:268
  93.4 1.2 broadcast_in_dim.127
  94.6 5.7 %all-to-all-start.2 = ((f16[32,144,128]{2,1,0:T(8,128)(2,1)}), f16[32,144,128]{2,1,0:T(8,128)(2,1)S(1)}, u32[]{:S(2)}, u32[]{:S(2)}) async-start(f16[32,144,128]{2,1,0:T(8,128)(2,1)} %broadcast_in_dim.127), calls=%async_computation.2 | async-start | bytes 2359296 | tf_op jit(solution)/shard_map/all_to_all | solution.py:158
  100.4 28.6 %all-to-all-done.2 = f16[32,144,128]{2,1,0:T(8,128)(2,1)S(1)} async-done(((f16[32,144,128]{2,1,0:T(8,128)(2,1)}), f16[32,144,128]{2,1,0:T(8,128)(2,1)S(1)}, u32[]{:S(2)}, u32[]{:S(2)}) %all-to-all-start.2) | async-done | bytes 1179680 | tf_op jit(solution)/shard_map/all_to_all | solution.py:158
  129.5 24.7 %orthonormal.1 = (bf16[1024,512]{1,0:T(8,128)(2,1)S(1)}, bf16[32,512]{1,0:T(8,128)(2,1)S(1)}, f32[32,512]{1,0:T(8,128)}) custom-call(s32[2]{0:T(128)S(1)} %pad_add_fusion.scalars_ref, f32[1024,128]{1,0:T(8,128)S(1)} %bitcast.57, f32[1024,128]{1,0:T(8,128)S(1)} %bitcast.56, f32[1024,128]{1,0:T(8,128)S(1)} %bitcast.55, f32[1024,128]{1,0:T(8,128)S(1)} %bitcast.54), custom_call_target="tpu_custom_call" | custom-call | flops 5000000000 | bytes 3145728 | tf_op jit(solution)/shard_map/orthonormal/pallas_call | solution.py:134
  154.1 1.2 collective-permute-done.4
  156.1 1.3 collective-permute-start.5
  157.5 5.2 %collective-permute-done.5 = bf16[2,32,512]{2,1,0:T(8,128)(2,1)S(1)} collective-permute-done((bf16[2,32,512]{2,1,0:T(8,128)(2,1)S(1)}, bf16[2,32,512]{2,1,0:T(8,128)(2,1)S(1)}, u32[]{:S(2)}, u32[]{:S(2)}) %collective-permute-start.5) | collective-permute-done | bytes 65568 | tf_op jit(solution)/shard_map/ppermute | solution.py:193
  162.7 1.6 gather_fusion.1
  164.3 6.0 %all-to-all-start.3 = ((bf16[32,32,512]{2,1,0:T(8,128)(2,1)}), bf16[32,32,512]{2,1,0:T(8,128)(2,1)}, u32[]{:S(2)}, u32[]{:S(2)}) async-start(bf16[32,32,512]{2,1,0:T(8,128)(2,1)} %gather_fusion.1), calls=%async_computation.3 | async-start | bytes 2097152 | tf_op jit(solution)/shard_map/all_to_all | solution.py:206
  170.3 2.3 %fusion.21 = bf16[1024,512]{0,1:T(8,128)(2,1)} fusion(bf16[1024,512]{1,0:T(8,128)(2,1)S(1)} %get-tuple-element.7, bf16[1,1,1024,1024]{3,2,1,0:T(8,128)(2,1)S(1)} %copy-done), kind=kOutput, calls=%fused_computation.19 | convolution fusion | flops 1074266112 | bytes 4194304 | tf_op jit(solution)/shard_map/dot_general | solution.py:276
  172.6 25.6 %all-to-all-done.3 = bf16[32,32,512]{2,1,0:T(8,128)(2,1)} async-done(((bf16[32,32,512]{2,1,0:T(8,128)(2,1)}), bf16[32,32,512]{2,1,0:T(8,128)(2,1)}, u32[]{:S(2)}, u32[]{:S(2)}) %all-to-all-start.3) | async-done | bytes 1048608 | tf_op jit(solution)/shard_map/all_to_all | solution.py:206
  198.3 3.3 %convolution_bitcast_fusion = f32[1,1,512,512]{3,2,1,0:T(8,128)} fusion(bf16[1024,512]{1,0:T(8,128)(2,1)} %bitcast.25, bf16[1024,512]{0,1:T(8,128)(2,1)} %fusion.21), kind=kOutput, calls=%fused_computation.20 | convolution fusion | flops 536870912 | bytes 3145728 | tf_op jit(solution)/shard_map/dot_general | solution.py:279
  (57 shorter events, 6.5 us)
Async XLA Ops:
  0.6 53.9 %copy-start = (bf16[1,1,1024,1024]{3,2,1,0:T(8,128)(2,1)S(1)}, bf16[1,1,1024,1024]{3,2,1,0:T(8,128)(2,1)}, u32[]{:S(2)}) copy-start(bf16[1,1,1024,1024]{3,2,1,0:T(8,128)(2,1)} %param.9) | copy-start | bytes 6291460
  0.6 1.8 collective-permute-start
  3.2 10.0 %collective-permute-start.3 = (bf16[2,16,1024]{2,1,0:T(8,128)(2,1)S(1)}, bf16[2,16,1024]{2,1,0:T(8,128)(2,1)S(1)}, u32[]{:S(2)}, u32[]{:S(2)}) collective-permute-start(bf16[2,16,1024]{2,1,0:T(8,128)(2,1)S(1)} %pad_maximum_fusion), channel_id=1, source_target_pairs={{0,192},{32,224},{64,0},{96,32},{128,64},{160,96},{192,128},{224,1... | collective-permute-start | bytes 196616 | tf_op jit(solution)/shard_map/ppermute | solution.py:193
  6.2 7.0 %collective-permute-start.2 = (bf16[2,16,1024]{2,1,0:T(8,128)(2,1)S(1)}, bf16[2,16,1024]{2,1,0:T(8,128)(2,1)S(1)}, u32[]{:S(2)}, u32[]{:S(2)}) collective-permute-start(bf16[2,16,1024]{2,1,0:T(8,128)(2,1)S(1)} %pad_maximum_fusion), channel_id=1, source_target_pairs={{0,128},{32,160},{64,192},{96,224},{128,0},{160,32},{192,64},{224,... | collective-permute-start | bytes 196616 | tf_op jit(solution)/shard_map/ppermute | solution.py:193
  6.8 6.3 %collective-permute-start.1 = (bf16[2,16,1024]{2,1,0:T(8,128)(2,1)S(1)}, bf16[2,16,1024]{2,1,0:T(8,128)(2,1)S(1)}, u32[]{:S(2)}, u32[]{:S(2)}) collective-permute-start(bf16[2,16,1024]{2,1,0:T(8,128)(2,1)S(1)} %pad_maximum_fusion), channel_id=1, source_target_pairs={{0,64},{32,96},{64,128},{96,160},{128,192},{160,224},{192,0},{224,... | collective-permute-start | bytes 196616 | tf_op jit(solution)/shard_map/ppermute | solution.py:193
  13.2 15.9 %copy-start.2 = (s32[8]{0:T(128)S(1)}, s32[8]{0:T(128)}, u32[]{:S(2)}) copy-start(s32[8]{0:T(128)} %param.11) | copy-start | bytes 100
  13.2 17.9 %copy-start.1 = (bf16[1,16,1024]{2,1,0:T(8,128)(2,1)S(1)}, bf16[1,16,1024]{2,1,0:T(8,128)(2,1)}, u32[]{:S(2)}) copy-start(bf16[1,16,1024]{2,1,0:T(8,128)(2,1)} %param.8) | copy-start | bytes 98308
  14.8 39.6 %all-to-all-start = ((bf16[32,16,1024]{2,1,0:T(8,128)(2,1)}), bf16[32,16,1024]{2,1,0:T(8,128)(2,1)S(1)}, u32[]{:S(2)}, u32[]{:S(2)}) async-start(bf16[32,16,1024]{2,1,0:T(8,128)(2,1)} %gather_fusion), calls=%async_computation | async-start | bytes 2097152 | tf_op jit(solution)/shard_map/all_to_all | solution.py:206
  54.5 1.3 copy-start.3
  59.1 5.7 %copy-start.4 = (s32[8]{0:T(128)S(1)}, s32[8]{0:T(128)}, u32[]{:S(2)}) copy-start(s32[8]{0:T(128)} %param.12) | copy-start | bytes 100
  59.1 32.5 %all-to-all-start.1 = ((bf16[32,32,512]{2,1,0:T(8,128)(2,1)}), bf16[32,32,512]{2,1,0:T(8,128)(2,1)S(1)}, u32[]{:S(2)}, u32[]{:S(2)}) async-start(bf16[32,32,512]{2,1,0:T(8,128)(2,1)} %bitcast.59), calls=%async_computation.1 | async-start | bytes 2097152 | tf_op jit(solution)/shard_map/all_to_all | solution.py:268
  94.6 34.5 %all-to-all-start.2 = ((f16[32,144,128]{2,1,0:T(8,128)(2,1)}), f16[32,144,128]{2,1,0:T(8,128)(2,1)S(1)}, u32[]{:S(2)}, u32[]{:S(2)}) async-start(f16[32,144,128]{2,1,0:T(8,128)(2,1)} %broadcast_in_dim.127), calls=%async_computation.2 | async-start | bytes 2359296 | tf_op jit(solution)/shard_map/all_to_all | solution.py:158
  154.1 1.2 collective-permute-start.4
  155.4 7.3 %collective-permute-start.7 = (bf16[2,32,512]{2,1,0:T(8,128)(2,1)S(1)}, bf16[2,32,512]{2,1,0:T(8,128)(2,1)S(1)}, u32[]{:S(2)}, u32[]{:S(2)}) collective-permute-start(bf16[2,32,512]{2,1,0:T(8,128)(2,1)S(1)} %pad_maximum_fusion.1), channel_id=1, source_target_pairs={{0,192},{32,224},{64,0},{96,32},{128,64},{160,96},{192,128},{224,1... | collective-permute-start | bytes 196616 | tf_op jit(solution)/shard_map/ppermute | solution.py:193
  155.5 7.2 %collective-permute-start.6 = (bf16[2,32,512]{2,1,0:T(8,128)(2,1)S(1)}, bf16[2,32,512]{2,1,0:T(8,128)(2,1)S(1)}, u32[]{:S(2)}, u32[]{:S(2)}) collective-permute-start(bf16[2,32,512]{2,1,0:T(8,128)(2,1)S(1)} %pad_maximum_fusion.1), channel_id=1, source_target_pairs={{0,128},{32,160},{64,192},{96,224},{128,0},{160,32},{192,64},{224,... | collective-permute-start | bytes 196616 | tf_op jit(solution)/shard_map/ppermute | solution.py:193
  156.1 6.5 %collective-permute-start.5 = (bf16[2,32,512]{2,1,0:T(8,128)(2,1)S(1)}, bf16[2,32,512]{2,1,0:T(8,128)(2,1)S(1)}, u32[]{:S(2)}, u32[]{:S(2)}) collective-permute-start(bf16[2,32,512]{2,1,0:T(8,128)(2,1)S(1)} %pad_maximum_fusion.1), channel_id=1, source_target_pairs={{0,64},{32,96},{64,128},{96,160},{128,192},{160,224},{192,0},{224,... | collective-permute-start | bytes 196616 | tf_op jit(solution)/shard_map/ppermute | solution.py:193
  164.3 34.0 %all-to-all-start.3 = ((bf16[32,32,512]{2,1,0:T(8,128)(2,1)}), bf16[32,32,512]{2,1,0:T(8,128)(2,1)}, u32[]{:S(2)}, u32[]{:S(2)}) async-start(bf16[32,32,512]{2,1,0:T(8,128)(2,1)} %gather_fusion.1), calls=%async_computation.3 | async-start | bytes 2097152 | tf_op jit(solution)/shard_map/all_to_all | solution.py:206

commit v6 on v5

--- a/solution.py
+++ b/solution.py
@@ -1,3 +1,5 @@
+import functools
+
 import jax
 import jax.numpy as jnp
 from jax import lax
@@ -5,14 +7,7 @@
 from jax.experimental.pallas import tpu as pltpu
 from jax.sharding import PartitionSpec as P
 
-HIGHEST = lax.Precision.HIGHEST
 LANE = 128
-
-
-def dot(a, b, ca, cb):
-    return lax.dot_general(
-        a, b, (((ca,), (cb,)), ((), ())), precision=HIGHEST, preferred_element_type=jnp.float32
-    )
 
 
 def dot3(a, b, ca, cb):
@@ -20,11 +15,24 @@
     a_high, b_high = a.astype(jnp.bfloat16), b.astype(jnp.bfloat16)
     a_low = (a - a_high.astype(jnp.float32)).astype(jnp.bfloat16)
     b_low = (b - b_high.astype(jnp.float32)).astype(jnp.bfloat16)
+    if a.shape[ca] < 2 * LANE:
+        return lax.dot_general(
+            jnp.concatenate([a_low, a_high, a_high], axis=ca),
+            jnp.concatenate([b_high, b_low, b_high], axis=cb),
+            dims,
+            preferred_element_type=jnp.float32,
+        )
     return (
         lax.dot_general(a_low, b_high, dims, preferred_element_type=jnp.float32)
         + lax.dot_general(a_high, b_low, dims, preferred_element_type=jnp.float32)
         + lax.dot_general(a_high, b_high, dims, preferred_element_type=jnp.float32)
     )
+
+
+def total(terms):
+    while len(terms) > 1:
+        terms = [sum(terms[i : i + 2][1:], terms[i]) for i in range(0, len(terms), 2)]
+    return terms[0]
 
 
 def factor_block(block):
@@ -57,7 +65,7 @@
                     for c in range(j + 1):
                         t = low[i, j] * m[j, c]
                         m[i, c] = m[i, c] - t if (i, c) in m else -t
-            rv = rw = None
+            tvs, tws = [], []
             mcols = []
             for j in range(8):
                 mc = jnp.zeros((8, LANE), jnp.float32)
@@ -65,8 +73,9 @@
                     mc = jnp.where(sub == i, m[i, j], mc)
                 tv = mc * jnp.broadcast_to(v[j:j + 1, :], (8, LANE))
                 tw = mc * jnp.broadcast_to(w[j:j + 1, :], (8, LANE))
-                rv = tv if rv is None else rv + tv
-                rw = tw if rw is None else rw + tw
+                tvs.append(tv)
+                tws.append(tw)
+            rv, rw = total(tvs), total(tws)
             out.append(rw)
             done_r.append(rv)
             done_w.append(rw)
@@ -75,82 +84,91 @@
                 rwb = [jnp.broadcast_to(rw[j:j + 1, :], (8, LANE)) for j in range(8)]
                 for h in range(g + 1, s + per):
                     raw = [jnp.broadcast_to(rows[h][:, 8 * g + j:8 * g + j + 1], (8, LANE)) for j in range(8)]
-                    nv, nw = rows[h], aug[h]
+                    nv, nw, subs_v, subs_w = rows[h], aug[h], [], []
                     for i in range(8):
-                        f = raw[0] * m[i, 0]
-                        for k in range(1, i + 1):
-                            f = f + raw[k] * m[i, k]
-                        nv = nv - f * rvb[i]
-                        nw = nw - f * rwb[i]
-                    rows[h], aug[h] = nv, nw
+                        f = total([raw[k] * m[i, k] for k in range(i + 1)])
+                        subs_v.append(f * rvb[i])
+                        subs_w.append(f * rwb[i])
+                    rows[h] = nv - total(subs_v)
+                    aug[h] = nw - total(subs_w)
         if s + per < groups:
             left = jnp.concatenate(done_r, axis=0)
             both = jnp.concatenate([left, jnp.concatenate(done_w, axis=0)], axis=1)
             rest = 8 * (s + per)
-            delta = dot(left, both, 0, 0)
+            delta = dot3(left, both, 0, 0)
             for h in range(s + per, groups):
                 rows[h] = rows[h] - delta[8 * h:8 * h + 8, :LANE]
                 aug[h] = aug[h] - delta[8 * h:8 * h + 8, LANE:]
     return jnp.concatenate(out, axis=0)
 
 
-def basis_kernel(scalars_ref, *refs):
-    blocks, (half_ref, tile_half_ref, kept_ref, q_ref, a_ref, t_ref) = refs[:-6], refs[-6:]
-    rows, width = t_ref.shape
+def basis_kernel(first, scalars_ref, *refs):
+    if first:
+        before_ref, given_ref = refs[:2]
+        blocks, (half_ref, kept_ref, q_ref, a_ref) = refs[2:-4], refs[-4:]
+        a_ref[first:, first:] = given_ref[first:, first:]
+    else:
+        blocks, (half_ref, kept_ref, q_ref, a_ref, t_ref) = refs[:-5], refs[-5:]
+    rows, count = half_ref.shape
+    width = a_ref.shape[0]
     kept, own = scalars_ref[0], scalars_ref[1]
-    for b, block in enumerate(blocks):
-        t_ref[:, b * LANE : (b + 1) * LANE] = block[...]
-    r_i = lax.broadcasted_iota(jnp.int32, (width, width), 0)
-    c_i = lax.broadcasted_iota(jnp.int32, (width, width), 1)
-    ones = jnp.where((r_i == c_i) & (c_i >= kept), 1.0, 0.0)
-    for lo in range(0, width, LANE):
-        hi = lo + LANE
-        a_ref[lo:hi, lo:] = dot3(t_ref[:, lo:hi], t_ref[:, lo:], 0, 0) + ones[lo:hi, lo:]
-    for lo in range(0, width, LANE):
-        hi = lo + LANE
+    if not first:
+        for b, block in enumerate(blocks):
+            t_ref[:, b * LANE : (b + 1) * LANE] = block[...]
+        r_i = lax.broadcasted_iota(jnp.int32, (width, width), 0)
+        c_i = lax.broadcasted_iota(jnp.int32, (width, width), 1)
+        ones = jnp.where((r_i == c_i) & (c_i >= kept), 1.0, 0.0)
+        for lo in range(0, width, LANE):
+            hi = lo + LANE
+            a_ref[lo:hi, lo:] = dot3(t_ref[:, lo:hi], t_ref[:, lo:], 0, 0) + ones[lo:hi, lo:]
+    for lo in range(first, first + count, LANE):
+        hi, at = lo + LANE, lo - first
         inv = factor_block(a_ref[lo:hi, lo:hi])
-        t = t_ref[:, lo:hi]
-        if lo:
-            t = t - dot3(q_ref[:, :lo], a_ref[:lo, lo:hi], 1, 0)
+        t = blocks[at // LANE][...]
+        if first:
+            t = t - dot3(before_ref[...], given_ref[:first, lo:hi], 1, 0)
+        if at:
+            t = t - dot3(q_ref[:, :at], a_ref[first:lo, lo:hi], 1, 0)
         q = dot3(t, inv, 1, 1)
-        q_ref[:, lo:hi] = q
-        half_ref[:, lo:hi] = q.astype(jnp.bfloat16)
+        q_ref[:, at : at + LANE] = q
+        half_ref[:, at : at + LANE] = q.astype(jnp.bfloat16)
         if hi < width:
-            r = dot(inv, a_ref[lo:hi, hi:], 1, 0)
+            r = dot3(inv, a_ref[lo:hi, hi:], 1, 0)
             a_ref[lo:hi, hi:] = r
             for c in range(hi, width, LANE):
-                a_ref[c : c + LANE, c:] = a_ref[c : c + LANE, c:] - dot(
+                a_ref[c : c + LANE, c:] = a_ref[c : c + LANE, c:] - dot3(
                     r[:, c - hi : c - hi + LANE], r[:, c - hi :], 0, 0
                 )
     tile = kept_ref.shape[0]
     mine = q_ref[pl.ds(pl.multiple_of(own * tile, tile), tile), :]
-    tile_half_ref[...] = mine.astype(jnp.bfloat16)
     kept_ref[...] = mine * float(rows) ** 0.5
 
 
-def orthonormal(blocks, scalars, tile):
-    rows, width = blocks[0].shape[0], len(blocks) * LANE
+def orthonormal(first, count, blocks, scalars, tile, state=()):
+    rows = blocks[0].shape[0]
+    width = state[1].shape[0] if state else len(blocks) * LANE
     vmem = pl.BlockSpec(memory_space=pltpu.VMEM)
+    shared = (
+        jax.ShapeDtypeStruct((rows, count), jnp.float32),
+        jax.ShapeDtypeStruct((width, width), jnp.float32),
+    )
+    scratch = [pltpu.VMEM(item.shape, item.dtype) for item in shared]
     return pl.pallas_call(
-        basis_kernel,
+        functools.partial(basis_kernel, first),
         out_shape=(
-            jax.ShapeDtypeStruct((rows, width), jnp.bfloat16),
-            jax.ShapeDtypeStruct((tile, width), jnp.bfloat16),
-            jax.ShapeDtypeStruct((tile, width), jnp.float32),
+            jax.ShapeDtypeStruct((rows, count), jnp.bfloat16),
+            jax.ShapeDtypeStruct((tile, count), jnp.float32),
+        )
+        + (() if state else shared),
+        in_specs=[pl.BlockSpec(memory_space=pltpu.SMEM)] + [vmem] * (len(blocks) + len(state)),
+        out_specs=(vmem,) * (2 if state else 4),
+        scratch_shapes=scratch if state else [pltpu.VMEM((rows, width), jnp.float32)],
+        compiler_params=pltpu.CompilerParams(vmem_limit_bytes=14 << 20),
+        cost_estimate=pl.CostEstimate(
+            flops=10_000_000_000, bytes_accessed=rows * width * 6, transcendentals=0
         ),
-        in_specs=[pl.BlockSpec(memory_space=pltpu.SMEM)] + [vmem] * len(blocks),
-        out_specs=(vmem,) * 3,
-        scratch_shapes=[
-            pltpu.VMEM((rows, width), jnp.float32),
-            pltpu.VMEM((width, width), jnp.float32),
-            pltpu.VMEM((rows, width), jnp.float32),
-        ],
-        compiler_params=pltpu.CompilerParams(vmem_limit_bytes=40 << 20),
-        cost_estimate=pl.CostEstimate(
-            flops=5_000_000_000, bytes_accessed=rows * width * 6, transcendentals=0
-        ),
-        name="orthonormal",
-    )(scalars, *blocks)
+        name="orthonormal_%d" % first,
+    )(scalars, *state, *blocks)
 
 
 def from_everyone(value, axis):
@@ -167,7 +185,7 @@
     scaled = (tile * jnp.exp2(12.0 - power)).astype(jnp.float16)
     sent = jnp.concatenate(
         [scaled[:, lo : lo + LANE] for lo in range(0, width, LANE)]
-        + [jnp.full((16, LANE), power, jnp.float32).astype(jnp.float16)],
+        + [jnp.full((8, LANE), power, jnp.float32).astype(jnp.float16)],
         axis=0,
     )
     got = from_everyone(sent, "op")
@@ -187,24 +205,40 @@
 
 def gather_sectors(value):
     size = lax.axis_size("sec")
-    other = lax.ppermute(value, "sec", [(i, i ^ 1) for i in range(size)])
-    pair = jnp.stack([value, other])
-    pairs = [pair] + [
-        lax.ppermute(pair, "sec", [(i, (i + 2 * step) % size) for i in range(size)])
-        for step in range(1, size // 2)
-    ]
-    return jnp.concatenate(pairs, axis=0)
+    chips = jnp.stack(
+        [value]
+        + [
+            lax.ppermute(value, "sec", [(i, (i + 2 * step) % size) for i in range(size)])
+            for step in range(1, size // 2)
+        ]
+    )
+    other = lax.ppermute(chips, "sec", [(i, i ^ 1) for i in range(size)])
+    return jnp.concatenate([chips, other], axis=0)
 
 
 def place_of(sector, own):
     chips = lax.axis_size("sec") // 2
-    return (own // 2 - sector // 2 + chips) % chips * 2 + (own + sector) % 2
+    return (own // 2 - sector // 2 + chips) % chips + (own + sector) % 2 * chips
 
 
 def fetch_pieces(own_slice, places):
     outgoing = jnp.take(gather_sectors(own_slice), places, axis=0, mode="clip")
     incoming = lax.all_to_all(outgoing, "op", 0, 0, tiled=True)
     return incoming.reshape(-1, incoming.shape[-1])
+
+
+def exchanged_sectors(values, wanted):
+    size = lax.axis_size("sec")
+    picked = []
+    for value in values:
+        if picked:
+            value, picked[-1] = lax.optimization_barrier((value, picked[-1]))
+        pieces = value.reshape(size, value.shape[0] // size, value.shape[1])
+        spread = lax.all_to_all(pieces, "sec", 0, 0, tiled=True)
+        picked.append(jnp.take(spread, wanted, axis=0, mode="clip"))
+    picked = jnp.concatenate(picked, axis=2)
+    got = lax.all_to_all(picked, "sec", 0, 0, tiled=True)
+    return got.reshape(-1, got.shape[2])
 
 
 def in_halves(value):
@@ -271,11 +305,23 @@
         jnp.sum(tiles.astype(jnp.float32), axis=0),
         jnp.float32(0.0),
     )
-    half, tile_half, kept_tile = orthonormal(gathered_rows(image), scalars, tile_rows)
+    images = gathered_rows(image)
+    first = kept_width // 2
+    half_a, kept_a, *state = orthonormal(0, first, images, scalars, tile_rows)
+    half_b, kept_b = orthonormal(
+        first, kept_width - first, images[first // LANE :], scalars, tile_rows, state
+    )
+    kept_tile = jnp.concatenate([kept_a, kept_b], axis=1)
+    source_basis = exchanged_sectors(
+        (half_a, half_b), lax.dynamic_index_in_dim(sources, op_index, 0, False)
+    )
     mapped = lax.optimization_barrier(
-        jnp.dot(blocks, half, preferred_element_type=jnp.float32).astype(jnp.bfloat16)
-    )
-    source_basis = fetch_pieces(tile_half, places)
+        jnp.dot(
+            blocks,
+            jnp.concatenate([half_a, half_b], axis=1),
+            preferred_element_type=jnp.float32,
+        ).astype(jnp.bfloat16)
+    )
     rotated = lax.dot_general(
         source_basis, mapped, (((0,), (0,)), ((), ())), preferred_element_type=jnp.float32
     )

time: 202 us -> 208 us (1.030)
  waiting for transfers between devices: 115 us -> 93.9 us
  blocking collectives: 0 us -> 14.7 us
  local copies, waits for them, and re-layouts: 7.4 us -> 15.9 us
  other arithmetic: 2.87 us -> 6.94 us
  Pallas kernels: 24.7 us -> 22.1 us
    all_to_all x2 -> x1, waiting for transfers between devices: 48.9 us -> 23.8 us  [fetch_pieces(): incoming = lax.all_to_all(outgoing, 'op', 0, 0, tiled=True)]
    all_to_all x0 -> x1, blocking collectives: none -> 14.7 us  [exchanged_sectors(): spread = lax.all_to_all(pieces, 'sec', 0, 0, tiled=True)]
    all_to_all x0 -> x2, waiting for transfers between devices: none -> 12 us  [the longest x1 12 us: exchanged_sectors(): got = lax.all_to_all(picked, 'sec', 0, 0, tiled=True)]
    all_to_all x0 -> x2, starting transfers between devices: none -> 8.61 us  [the longest x1 4.37 us: exchanged_sectors(): spread = lax.all_to_all(pieces, 'sec', 0, 0, tiled=True)]
    ppermute x8 -> x4, waiting for transfers between devices: 11.8 us -> 4.12 us  [the longest x3 2.82 us: gather_sectors(): lax.ppermute(value, 'sec', [(i, (i + 2 * step) % size) for i in range(siz...]
    unnamed x23 -> x33, local copies, waits for them, and re-layouts: 1.1 us -> 7.32 us
    all_to_all x2 -> x1, starting transfers between devices: 17.6 us -> 11.6 us  [fetch_pieces(): incoming = lax.all_to_all(outgoing, 'op', 0, 0, tiled=True)]
    gather x0 -> x2, local copies, waits for them, and re-layouts: none -> 3.81 us  [exchanged_sectors(): picked.append(jnp.take(spread, wanted, axis=0, mode='clip'))]
  transfers between devices with their start and end apart: 12 -> 9, of which waited for: 7 -> 7; matrix products, arithmetic and copies ran while one was open for 3% -> 4% of each run, Pallas kernels for 0% -> 5%
where the time goes in v6:
time: 208 us; the launch traced here: 207 us
  waiting for transfers between devices  93.9 us (45%)
  starting transfers between devices  36.3 us (17%)
  Pallas kernels  22.1 us (11%)
  local copies, waits for them, and re-layouts  15.9 us (8%)
  blocking collectives  14.7 us (7%)
  matrix products  11.2 us (5%)
  other arithmetic  6.94 us (3%)
  between operations  5.5 us (3%)
    all_to_all x1, waiting for transfers between devices, from_everyone(): lax.all_to_all(jnp.broadcast_to(value[None], (size, *value.shape)), axis,...  27.9 us
    all_to_all x1, waiting for transfers between devices, body(): lax.all_to_all(part.reshape(ops, tile_rows, kept_width), 'op', 0, 0, tile...  26.1 us
    all_to_all x1, waiting for transfers between devices, fetch_pieces(): incoming = lax.all_to_all(outgoing, 'op', 0, 0, tiled=True)  23.8 us
    pallas_call x2, Pallas kernels, orthonormal(): pl.pallas_call(functools.partial(basis_kernel, first), out_shape=(jax.Sha...  22.1 us
    all_to_all x1, blocking collectives, exchanged_sectors(): spread = lax.all_to_all(pieces, 'sec', 0, 0, tiled=True)  14.7 us
    all_to_all x1, waiting for transfers between devices, exchanged_sectors(): got = lax.all_to_all(picked, 'sec', 0, 0, tiled=True)  12 us
    all_to_all x1, starting transfers between devices, fetch_pieces(): incoming = lax.all_to_all(outgoing, 'op', 0, 0, tiled=True)  11.6 us
    unnamed x33, local copies, waits for them, and re-layouts  7.32 us
  transfers between devices with their start and end apart: 9, of which 7 were waited for; matrix products, arithmetic and copies ran while one was open for 4% of the time, Pallas kernels for 5%

profile of v6, /device:TPU:2, one launch (start us, length us, event | category | flops | bytes accessed | tf_op | source)
XLA Modules:
  0.0 206.5 jit_solution(2840923893525577585)
XLA Ops:
  0.6 3.1 %collective-permute-start.2 = (bf16[16,1024]{1,0:T(8,128)(2,1)}, bf16[16,1024]{1,0:T(8,128)(2,1)S(1)}, u32[]{:S(2)}, u32[]{:S(2)}) collective-permute-start(bf16[16,1024]{1,0:T(8,128)(2,1)} %bitcast.65), channel_id=1, source_target_pairs={{0,192},{32,224},{64,0},{96,32},{128,64},{160,96},{192,128},{224,1... | collective-permute-start | bytes 98312 | tf_op jit(solution)/shard_map/ppermute | solution.py:211
  6.9 2.5 %collective-permute-done.1 = bf16[16,1024]{1,0:T(8,128)(2,1)S(1)} collective-permute-done((bf16[16,1024]{1,0:T(8,128)(2,1)}, bf16[16,1024]{1,0:T(8,128)(2,1)S(1)}, u32[]{:S(2)}, u32[]{:S(2)}) %collective-permute-start.1) | collective-permute-done | bytes 32800 | tf_op jit(solution)/shard_map/ppermute | solution.py:211
  10.6 1.3 collective-permute-done.3
  12.0 1.6 gather_fusion
  13.6 11.6 %all-to-all-start = ((bf16[32,16,1024]{2,1,0:T(8,128)(2,1)}), bf16[32,16,1024]{2,1,0:T(8,128)(2,1)S(1)}, u32[]{:S(2)}, u32[]{:S(2)}) async-start(bf16[32,16,1024]{2,1,0:T(8,128)(2,1)} %gather_fusion), calls=%async_computation | async-start | bytes 2097152 | tf_op jit(solution)/shard_map/all_to_all | solution.py:226
  29.7 23.8 %all-to-all-done = bf16[32,16,1024]{2,1,0:T(8,128)(2,1)S(1)} async-done(((bf16[32,16,1024]{2,1,0:T(8,128)(2,1)}), bf16[32,16,1024]{2,1,0:T(8,128)(2,1)S(1)}, u32[]{:S(2)}, u32[]{:S(2)}) %all-to-all-start) | async-done | bytes 1048608 | tf_op jit(solution)/shard_map/all_to_all | solution.py:226
  53.7 1.3 fusion.12
  55.8 2.5 %fusion.18 = bf16[1024,512]{1,0:T(8,128)(2,1)} fusion(bf16[16,1024]{1,0:T(8,128)(2,1)S(1)} %broadcast_select_fusion.1, bf16[512,1024]{1,0:T(8,128)(2,1)S(1)} %fusion.12, bf16[528,512]{1,0:T(8,128)(2,1)S(1)} %get-tuple-element.73, bf16[528,512]{1,0:T(8,128)(2,1)S(1)} %get-tuple-element.74), kind=kOutput, calls=%fused_computation.18 | convolution fusion | flops 1118633984 | bytes 3211264 | tf_op jit(solution)/shard_map/dot_general | solution.py:250
  58.3 5.7 %all-to-all-start.1 = ((bf16[32,32,512]{2,1,0:T(8,128)(2,1)}), bf16[32,32,512]{2,1,0:T(8,128)(2,1)S(1)}, u32[]{:S(2)}, u32[]{:S(2)}) async-start(bf16[32,32,512]{2,1,0:T(8,128)(2,1)} %bitcast.63), calls=%async_computation.1 | async-start | bytes 2097152 | tf_op jit(solution)/shard_map/all_to_all | solution.py:302
  65.2 26.1 %all-to-all-done.1 = bf16[32,32,512]{2,1,0:T(8,128)(2,1)S(1)} async-done(((bf16[32,32,512]{2,1,0:T(8,128)(2,1)}), bf16[32,32,512]{2,1,0:T(8,128)(2,1)S(1)}, u32[]{:S(2)}, u32[]{:S(2)}) %all-to-all-start.1) | async-done | bytes 1048608 | tf_op jit(solution)/shard_map/all_to_all | solution.py:302
  94.2 5.6 %all-to-all-start.2 = ((f16[32,136,128]{2,1,0:T(8,128)(2,1)}), f16[32,136,128]{2,1,0:T(8,128)(2,1)S(1)}, u32[]{:S(2)}, u32[]{:S(2)}) async-start(f16[32,136,128]{2,1,0:T(8,128)(2,1)} %broadcast_in_dim.130), calls=%async_computation.2 | async-start | bytes 2228224 | tf_op jit(solution)/shard_map/all_to_all | solution.py:176
  100.1 27.9 %all-to-all-done.2 = f16[32,136,128]{2,1,0:T(8,128)(2,1)S(1)} async-done(((f16[32,136,128]{2,1,0:T(8,128)(2,1)}), f16[32,136,128]{2,1,0:T(8,128)(2,1)S(1)}, u32[]{:S(2)}, u32[]{:S(2)}) %all-to-all-start.2) | async-done | bytes 1114144 | tf_op jit(solution)/shard_map/all_to_all | solution.py:176
  128.9 1.4 convert_multiply_fusion
  130.4 11.7 %orthonormal_0.1 = (bf16[1024,256]{1,0:T(8,128)(2,1)}, f32[32,256]{1,0:T(8,128)S(1)}, f32[1024,256]{1,0:T(8,128)S(1)}, f32[512,512]{1,0:T(8,128)S(1)}) custom-call(s32[2]{0:T(128)S(1)} %pad_add_fusion.scalars_ref, f32[1024,128]{1,0:T(8,128)S(1)} %bitcast.62, f32[1024,128]{1,0:T(8,128)S(1)} %bitcast.61, f32[1024,128]{1,0:T(8,128)S(1)} %bitcast.59, ...), custom_call_target="tpu_custom_call" | custom-call | flops 10000000000 | bytes 3145728 | tf_op jit(solution)/shard_map/orthonormal_0/pallas_call | solution.py:156
  144.1 4.4 %all-to-all-start.3 = ((bf16[8,128,256]{2,1,0:T(8,128)(2,1)}), bf16[8,128,256]{2,1,0:T(8,128)(2,1)}, u32[]{:S(2)}, u32[]{:S(2)}) async-start(bf16[8,128,256]{2,1,0:T(8,128)(2,1)} %bitcast.25), calls=%async_computation.3 | async-start | bytes 1048576 | tf_op jit(solution)/shard_map/all_to_all | solution.py:237
  152.0 10.4 %orthonormal_256.1 = (bf16[1024,256]{1,0:T(8,128)(2,1)S(1)}, f32[32,256]{1,0:T(8,128)S(1)}) custom-call(s32[2]{0:T(128)S(1)} %pad_add_fusion.scalars_ref, f32[1024,256]{1,0:T(8,128)S(1)} %copy-done.4, f32[512,512]{1,0:T(8,128)S(1)} %copy-done.6, f32[1024,128]{1,0:T(8,128)S(1)} %bitcast.60, f32[1024,128]{1,0:T(8,128)S(1)} %bitcast.58), custom_call_target="tpu_custom_call" | custom-call | flops 10000000000 | bytes 3145728 | tf_op jit(solution)/shard_map/orthonormal_256/pallas_call | solution.py:156
  162.3 2.4 %gather_fusion.1 = bf16[8,128,256]{2,1,0:T(8,128)(2,1)} fusion(bf16[8,128,256]{2,1,0:T(8,128)(2,1)} %all-to-all-done.3, s32[1024]{0:T(1024)S(1)} %pad_clamp_fusion), kind=kCustom, calls=%fused_computation.1 | custom fusion | bytes 1048608 | tf_op jit(solution)/shard_map/jit(_take)/gather | solution.py:238
  164.8 14.7 %all_to_all.30 = bf16[8,128,256]{2,1,0:T(8,128)(2,1)S(1)} all-to-all(bf16[8,128,256]{2,1,0:T(8,128)(2,1)S(1)} %bitcast.56), channel_id=1, replica_groups=mesh['sec'=8,'op'=32] {'sec'}, dimensions={0} | all-to-all | bytes 1048576 | tf_op jit(solution)/shard_map/all_to_all | solution.py:237
  179.4 1.4 gather_fusion.2
  180.8 2.2 %pad_maximum_fusion = bf16[8,128,512]{2,1,0:T(8,128)(2,1)} fusion(bf16[8,128,256]{2,1,0:T(8,128)(2,1)} %gather_fusion.2, bf16[8,128,256]{2,1,0:T(8,128)(2,1)} %gather_fusion.1), kind=kLoop, calls=%fused_computation.29 | loop fusion | flops 2097152 | bytes 2097152 | tf_op jit(solution)/shard_map/concatenate | solution.py:239
  183.1 4.2 %all-to-all-start.5 = ((bf16[8,128,512]{2,1,0:T(8,128)(2,1)}), bf16[8,128,512]{2,1,0:T(8,128)(2,1)}, u32[]{:S(2)}, u32[]{:S(2)}) async-start(bf16[8,128,512]{2,1,0:T(8,128)(2,1)} %pad_maximum_fusion), calls=%async_computation.5 | async-start | bytes 2097152 | tf_op jit(solution)/shard_map/all_to_all | solution.py:240
  187.3 3.3 %fusion.21 = bf16[1024,512]{0,1:T(8,128)(2,1)} fusion(bf16[1,1,1024,1024]{3,2,1,0:T(8,128)(2,1)S(1)} %copy-done, bf16[1024,256]{1,0:T(8,128)(2,1)S(1)} %get-tuple-element.17, bf16[1024,256]{1,0:T(8,128)(2,1)} %get-tuple-element.15), kind=kOutput, calls=%fused_computation.20 | convolution fusion | flops 1076363264 | bytes 4194304 | tf_op jit(solution)/shard_map/dot_general | solution.py:319
  191.3 12.0 %all-to-all-done.5 = bf16[8,128,512]{2,1,0:T(8,128)(2,1)} async-done(((bf16[8,128,512]{2,1,0:T(8,128)(2,1)}), bf16[8,128,512]{2,1,0:T(8,128)(2,1)}, u32[]{:S(2)}, u32[]{:S(2)}) %all-to-all-start.5) | async-done | bytes 1048608 | tf_op jit(solution)/shard_map/all_to_all | solution.py:240
  203.3 3.3 %convolution_bitcast_fusion = f32[1,1,512,512]{3,2,1,0:T(8,128)} fusion(bf16[1024,512]{1,0:T(8,128)(2,1)} %bitcast.27, bf16[1024,512]{0,1:T(8,128)(2,1)} %fusion.21), kind=kOutput, calls=%fused_computation.21 | convolution fusion | flops 536870912 | bytes 3145728 | tf_op jit(solution)/shard_map/dot_general | solution.py:325
  (66 shorter events, 16.7 us)
Async XLA Ops:
  0.6 53.0 %copy-start = (bf16[1,1,1024,1024]{3,2,1,0:T(8,128)(2,1)S(1)}, bf16[1,1,1024,1024]{3,2,1,0:T(8,128)(2,1)}, u32[]{:S(2)}) copy-start(bf16[1,1,1024,1024]{3,2,1,0:T(8,128)(2,1)} %param.9) | copy-start | bytes 6291460
  0.6 6.2 %collective-permute-start.2 = (bf16[16,1024]{1,0:T(8,128)(2,1)}, bf16[16,1024]{1,0:T(8,128)(2,1)S(1)}, u32[]{:S(2)}, u32[]{:S(2)}) collective-permute-start(bf16[16,1024]{1,0:T(8,128)(2,1)} %bitcast.65), channel_id=1, source_target_pairs={{0,192},{32,224},{64,0},{96,32},{128,64},{160,96},{192,128},{224,1... | collective-permute-start | bytes 98312 | tf_op jit(solution)/shard_map/ppermute | solution.py:211
  3.7 5.6 %collective-permute-start.1 = (bf16[16,1024]{1,0:T(8,128)(2,1)}, bf16[16,1024]{1,0:T(8,128)(2,1)S(1)}, u32[]{:S(2)}, u32[]{:S(2)}) collective-permute-start(bf16[16,1024]{1,0:T(8,128)(2,1)} %bitcast.66), channel_id=1, source_target_pairs={{0,128},{32,160},{64,192},{96,224},{128,0},{160,32},{192,64},{224,... | collective-permute-start | bytes 98312 | tf_op jit(solution)/shard_map/ppermute | solution.py:211
  4.4 5.4 %collective-permute-start = (bf16[16,1024]{1,0:T(8,128)(2,1)}, bf16[16,1024]{1,0:T(8,128)(2,1)S(1)}, u32[]{:S(2)}, u32[]{:S(2)}) collective-permute-start(bf16[16,1024]{1,0:T(8,128)(2,1)} %bitcast.67), channel_id=1, source_target_pairs={{0,64},{32,96},{64,128},{96,160},{128,192},{160,224},{192,0},{224,... | collective-permute-start | bytes 98312 | tf_op jit(solution)/shard_map/ppermute | solution.py:211
  10.5 1.4 collective-permute-start.3
  11.9 15.8 %copy-start.9 = (s32[8]{0:T(128)S(1)}, s32[8]{0:T(128)}, u32[]{:S(2)}) copy-start(s32[8]{0:T(128)} %param.11) | copy-start | bytes 100
  12.0 17.8 %copy-start.8 = (bf16[1,16,1024]{2,1,0:T(8,128)(2,1)S(1)}, bf16[1,16,1024]{2,1,0:T(8,128)(2,1)}, u32[]{:S(2)}) copy-start(bf16[1,16,1024]{2,1,0:T(8,128)(2,1)} %param.8) | copy-start | bytes 98308
  13.6 40.0 %all-to-all-start = ((bf16[32,16,1024]{2,1,0:T(8,128)(2,1)}), bf16[32,16,1024]{2,1,0:T(8,128)(2,1)S(1)}, u32[]{:S(2)}, u32[]{:S(2)}) async-start(bf16[32,16,1024]{2,1,0:T(8,128)(2,1)} %gather_fusion), calls=%async_computation | async-start | bytes 2097152 | tf_op jit(solution)/shard_map/all_to_all | solution.py:226
  53.6 1.3 copy-start.10
  58.3 5.7 %copy-start.11 = (s32[8]{0:T(128)S(1)}, s32[8]{0:T(128)}, u32[]{:S(2)}) copy-start(s32[8]{0:T(128)} %param.12) | copy-start | bytes 100
  58.3 33.0 %all-to-all-start.1 = ((bf16[32,32,512]{2,1,0:T(8,128)(2,1)}), bf16[32,32,512]{2,1,0:T(8,128)(2,1)S(1)}, u32[]{:S(2)}, u32[]{:S(2)}) async-start(bf16[32,32,512]{2,1,0:T(8,128)(2,1)} %bitcast.63), calls=%async_computation.1 | async-start | bytes 2097152 | tf_op jit(solution)/shard_map/all_to_all | solution.py:302
  94.2 33.7 %all-to-all-start.2 = ((f16[32,136,128]{2,1,0:T(8,128)(2,1)}), f16[32,136,128]{2,1,0:T(8,128)(2,1)S(1)}, u32[]{:S(2)}, u32[]{:S(2)}) async-start(f16[32,136,128]{2,1,0:T(8,128)(2,1)} %broadcast_in_dim.130), calls=%async_computation.2 | async-start | bytes 2228224 | tf_op jit(solution)/shard_map/all_to_all | solution.py:176
  127.9 1.0 copy-start.7
  130.4 11.8 %copy-start.1 = (f32[32,32,128]{2,1,0:T(8,128)}, f32[32,32,128]{2,1,0:T(8,128)S(1)}, u32[]{:S(2)}) copy-start(f32[32,32,128]{2,1,0:T(8,128)S(1)} %get-tuple-element.78) | copy-start | bytes 1572868
  142.1 1.0 copy-start.3
  143.1 1.0 copy-start.5
  144.1 18.2 %all-to-all-start.3 = ((bf16[8,128,256]{2,1,0:T(8,128)(2,1)}), bf16[8,128,256]{2,1,0:T(8,128)(2,1)}, u32[]{:S(2)}, u32[]{:S(2)}) async-start(bf16[8,128,256]{2,1,0:T(8,128)(2,1)} %bitcast.25), calls=%async_computation.3 | async-start | bytes 1048576 | tf_op jit(solution)/shard_map/all_to_all | solution.py:237
  148.5 1.0 copy-start.2
  149.5 1.2 copy-start.4
  150.7 1.2 copy-start.6
  183.1 20.2 %all-to-all-start.5 = ((bf16[8,128,512]{2,1,0:T(8,128)(2,1)}), bf16[8,128,512]{2,1,0:T(8,128)(2,1)}, u32[]{:S(2)}, u32[]{:S(2)}) async-start(bf16[8,128,512]{2,1,0:T(8,128)(2,1)} %pad_maximum_fusion), calls=%async_computation.5 | async-start | bytes 2097152 | tf_op jit(solution)/shard_map/all_to_all | solution.py:240
